TPU v7x, 256 devices: a whole 4x4x8 slice. The times are simulated.
256 devices in a mesh: batch: 16 (over z, core), seq: 16 (over y, x).
Axes of the slice: x: 4, y: 4, z: 8, core: 2. Of those that a mesh axis runs over, the one named last changes fastest.
Arguments:
- token_cond: bfloat16 [131072, 768], P(('batch', 'seq')), parts along dimension 0, may hold values from -6 to 6
- atom_feat: bfloat16 [1048576, 128], P(('batch', 'seq')), parts along dimension 0, may hold values from -16 to 16
- atom_counts: int32 [131072], P(('batch', 'seq')), parts along dimension 0, may hold values from 1 to 24, as said below
- w_token: bfloat16 [768, 128], replicated, may hold values from -0.21875 to 0.21875
- w_query: bfloat16 [128, 128], replicated, may hold values from -0.5 to 0.5
- w_key: bfloat16 [128, 128], replicated, may hold values from -0.5 to 0.5
- w_value: bfloat16 [128, 128], replicated, may hold values from -0.5 to 0.5
- w_out: bfloat16 [128, 128], replicated, may hold values from -0.5 to 0.5
- w_back: bfloat16 [128, 768], replicated, may hold values from -0.5 to 0.5
Outputs:
- token_out: bfloat16 [131072, 768], P(('batch', 'seq')), parts along dimension 0
- atom_out: bfloat16 [1048576, 128], P(('batch', 'seq')), parts along dimension 0
There are 16 independent parts, one for each index of `batch`. A program takes and returns all parts, laid end to end along the dimension named above; an argument that names none is the same for every part. Nothing has to cross between parts.
Inputs may be any that keep to these rules, and one draw needn't show every extreme that they name: `atom_counts`: every token has at least one atom and the counts of one complex sum to 65536. For every k, the atoms k * 4096 to (k + 1) * 4096 - 1 belong to tokens of (k - 1) * 512 to (k + 2) * 512 - 1.
All inputs are finite; a program needn't handle non-finite values.
Results may differ from a plain program's by a relative error of at most 0.0095.
The roundings to bfloat16 on the way count: a program that leaves them out, or rounds other values in their place, can miss the bound.
Values may be sent and summed in bfloat16 or wider, within the bound.
No kernel may reach another device: no remote copies, remote signals or barrier semaphores. Data moves between devices by JAX's collectives and lax.ppermute only.
A program may use at most 128 MiB of HBM per device.

v0:
```python
import math

import jax
import jax.numpy as jnp
from jax import lax
from jax.experimental import pallas as pl
from jax.experimental.pallas import tpu as pltpu
from jax.sharding import PartitionSpec as P

BF16 = jnp.bfloat16
F32 = jnp.float32
HEADS = 4
QBLOCK = 32
KEYS = 128
HALO = 48
LANES = 128
PAD = 64
NT = (((1,), (1,)), ((), ()))
TN = (((0,), (0,)), ((), ()))


def plan_kernel(counts_ref, starts_ref, ends_ref, tiles_ref, spad, epad, *, atoms, pad_chunks, chunks):
    position = lax.axis_index("seq")
    rows = counts_ref.shape[0]
    counts = counts_ref[...].astype(F32)
    exact = counts.astype(BF16)
    up_to = (
        lax.broadcasted_iota(jnp.int32, (LANES, LANES), 0)
        <= lax.broadcasted_iota(jnp.int32, (LANES, LANES), 1)
    )
    within = jnp.dot(exact, up_to.astype(F32).astype(BF16), preferred_element_type=F32)
    before = (
        lax.broadcasted_iota(jnp.int32, (rows, rows), 1)
        < lax.broadcasted_iota(jnp.int32, (rows, rows), 0)
    )
    ahead = jnp.dot(before.astype(F32).astype(BF16), exact, preferred_element_type=F32)
    ends = (within + jnp.sum(ahead, axis=1, keepdims=True)).astype(jnp.int32) - position * atoms
    far = 1 << 24
    spad[0:8, :] = jnp.full((8, LANES), -far, jnp.int32)
    epad[0:8, :] = jnp.full((8, LANES), -far, jnp.int32)
    spad[8 + rows : 16 + rows, :] = jnp.full((8, LANES), far, jnp.int32)
    epad[8 + rows : 16 + rows, :] = jnp.full((8, LANES), far, jnp.int32)
    spad[8 : 8 + rows, :] = ends - counts_ref[...]
    epad[8 : 8 + rows, :] = ends
    first = position * (chunks // 3) - (chunks // 3) - pad_chunks + 8
    near_ends = epad[pl.ds(first, 16), :]
    starts_ref[...] = spad[pl.ds(first, 16), :]
    ends_ref[...] = near_ends
    lane = lax.broadcasted_iota(jnp.int32, (16, LANES), 1)
    row = lax.broadcasted_iota(jnp.int32, (16, LANES), 0)
    tiles = atoms // LANES
    tile_start = jnp.where(lane == tiles, -HALO, lane * LANES)
    tile_start = jnp.where(lane == tiles + 1, atoms, tile_start)
    total = chunks + 2 * pad_chunks
    passed = (near_ends[:, LANES - 1 :] <= tile_start) & (row < total)
    index = jnp.sum(passed.astype(F32), axis=0, keepdims=True).astype(jnp.int32)
    index = jnp.minimum(index, total - 2)
    tiles_ref[...] = jnp.broadcast_to(index, (8, LANES))


def atom_kernel(
    tiles_ref, starts_ref, ends_ref, feat_ref, fleft_ref, fright_ref, far_left_ref, left_ref,
    own_ref, right_ref, far_right_ref, wqkv_ref, wout_ref,
    out_ref, send_a_ref, send_b_ref, mine_ref,
    table, member, xs, qs, ks, vs, os, acc,
    *, atoms, tok, ndev,
):
    position = lax.axis_index("seq")
    tiles = atoms // LANES
    edge = far_left_ref.shape[0]
    zero = jnp.zeros((LANES - edge, LANES), BF16)
    base = LANES
    table[0 : base - edge, :] = zero
    table[base - edge : base, :] = far_left_ref[...]
    table[base : base + tok, :] = left_ref[...]
    table[base + tok : base + 2 * tok, :] = own_ref[...]
    table[base + 2 * tok : base + 3 * tok, :] = right_ref[...]
    table[base + 3 * tok : base + 3 * tok + edge, :] = far_right_ref[...]
    table[base + 3 * tok + edge :, :] = zero

    def members(chunk, first, height):
        ids = lax.broadcasted_iota(jnp.int32, (height, 2 * LANES), 0)
        lo = jnp.concatenate([starts_ref[pl.ds(chunk, 1), :], starts_ref[pl.ds(chunk + 1, 1), :]], axis=1) - first
        hi = jnp.concatenate([ends_ref[pl.ds(chunk, 1), :], ends_ref[pl.ds(chunk + 1, 1), :]], axis=1) - first
        return jnp.where((ids >= lo) & (ids < hi), 1.0, 0.0).astype(BF16)

    def rows_of(chunk, hit):
        window = table[pl.ds(pl.multiple_of(chunk * LANES, LANES), 2 * LANES), :]
        return jnp.dot(hit, window, preferred_element_type=F32)

    def halo_rows(index, first, feat):
        chunk = tiles_ref[0, index]
        got = rows_of(chunk, members(chunk, first, HALO))
        return (feat.astype(F32) + got).astype(BF16)

    xs[0 : PAD - HALO, :] = jnp.zeros((PAD - HALO, LANES), BF16)
    xs[PAD + atoms + HALO :, :] = jnp.zeros((PAD - HALO, LANES), BF16)
    xs[PAD - HALO : PAD, :] = halo_rows(tiles, -HALO, fleft_ref[...])
    xs[PAD + atoms : PAD + atoms + HALO, :] = halo_rows(tiles + 1, atoms, fright_ref[...])

    group = 4

    def gather(i, carry):
        for j in range(group):
            t = i * group + j
            at = pl.multiple_of(t * LANES, LANES)
            chunk = tiles_ref[0, t]
            hit = members(chunk, at, LANES)
            member[pl.ds(at, LANES), :] = hit
            x = feat_ref[pl.ds(at, LANES), :].astype(F32) + rows_of(chunk, hit)
            xs[pl.ds(at + PAD, LANES), :] = x.astype(BF16)
        return carry

    lax.fori_loop(0, tiles // group, gather, 0)

    span = (atoms + 2 * PAD) // 11

    def project(i, carry):
        at = pl.multiple_of(i * span, 128)
        r = jnp.dot(xs[pl.ds(at, span), :], wqkv_ref[...], preferred_element_type=F32).astype(BF16)
        qs[pl.ds(at, span), :] = r[:, :LANES]
        ks[pl.ds(at, span), :] = r[:, LANES : 2 * LANES]
        vs[pl.ds(at, span), :LANES] = r[:, 2 * LANES :]
        vs[pl.ds(at, span), LANES:] = jnp.ones((span, LANES), BF16)
        return carry

    lax.fori_loop(0, 11, project, 0)

    @pl.when(position == 0)
    def _():
        ks[PAD - HALO : PAD, :] = jnp.broadcast_to(ks[PAD : PAD + 1, :].astype(F32), (HALO, LANES)).astype(BF16)
        vs[PAD - HALO : PAD, :] = jnp.zeros((HALO, 2 * LANES), BF16)

    @pl.when(position == ndev - 1)
    def _():
        last = PAD + atoms
        ks[last : last + HALO, :] = jnp.broadcast_to(ks[last - 1 : last, :].astype(F32), (HALO, LANES)).astype(BF16)
        vs[last : last + HALO, :] = jnp.zeros((HALO, 2 * LANES), BF16)

    row_head = lax.broadcasted_iota(jnp.int32, (LANES, LANES), 0) // QBLOCK
    lane_head = lax.broadcasted_iota(jnp.int32, (LANES, LANES), 1) // (LANES // HEADS)
    same = (row_head == lane_head).astype(F32).astype(BF16)
    lanes = lax.broadcasted_iota(jnp.int32, (QBLOCK, LANES), 1) // (LANES // HEADS)
    scale = math.log2(math.e) / math.sqrt(LANES // HEADS)

    def diagonal(full):
        parts = [full[h * QBLOCK : (h + 1) * QBLOCK, :] for h in range(HEADS)]
        out = parts[HEADS - 1]
        for h in range(HEADS - 2, -1, -1):
            out = jnp.where(lanes == h, parts[h], out)
        return out

    per = 8

    def attend(i, carry):
        for j in range(per):
            at = pl.multiple_of((i * per + j) * QBLOCK, QBLOCK)
            q = qs[pl.ds(at + PAD, QBLOCK), :]
            q = jnp.concatenate([q] * HEADS, axis=0) * same
            key = ks[pl.ds(at + PAD - HALO, KEYS), :]
            s = lax.dot_general(q, key, NT, preferred_element_type=F32)
            top = jnp.max(s, axis=1, keepdims=True)
            p = jnp.exp2((s - top) * scale).astype(BF16)
            o = jnp.dot(p, vs[pl.ds(at + PAD - HALO, KEYS), :], preferred_element_type=F32)
            o = diagonal(o[:, :LANES]) / diagonal(o[:, LANES:])
            os[pl.ds(at, QBLOCK), :] = o.astype(BF16)
        return carry

    lax.fori_loop(0, atoms // QBLOCK // per, attend, 0)

    tall = 512

    def finish(i, carry):
        at = pl.multiple_of(i * tall, tall)
        r = jnp.dot(os[pl.ds(at, tall), :], wout_ref[...], preferred_element_type=F32)
        out_ref[pl.ds(at, tall), :] = (xs[pl.ds(at + PAD, tall), :].astype(F32) + r).astype(BF16)
        return carry

    lax.fori_loop(0, atoms // tall, finish, 0)

    acc[...] = jnp.zeros_like(acc)

    def pool(i, carry):
        for j in range(group):
            t = i * group + j
            at = pl.multiple_of(t * LANES, LANES)
            chunk = tiles_ref[0, t]
            part = lax.dot_general(
                member[pl.ds(at, LANES), :], out_ref[pl.ds(at, LANES), :], TN, preferred_element_type=F32
            )
            to = pl.ds(pl.multiple_of(chunk * LANES, LANES), 2 * LANES)
            acc[to, :] = acc[to, :] + part
        return carry

    lax.fori_loop(0, tiles // group, pool, 0)
    odd = lax.rem(position, 2)
    from_a = pl.multiple_of(base + (1 - odd) * 2 * tok, LANES)
    from_b = pl.multiple_of(base + odd * 2 * tok, LANES)
    send_a_ref[...] = acc[pl.ds(from_a, tok), :].astype(BF16)
    send_b_ref[...] = acc[pl.ds(from_b, tok), :].astype(BF16)
    mine_ref[...] = acc[base + tok : base + 2 * tok, :]


def shards(token_cond, atom_feat, atom_counts, w_token, w_query, w_key, w_value, w_out, w_back):
    tok = token_cond.shape[0]
    atoms, width = atom_feat.shape
    ndev = lax.axis_size("seq")

    def shifted(x, by):
        return lax.ppermute(x, "seq", [(i, (i + by) % ndev) for i in range(ndev)])

    counts = atom_counts.reshape(tok // LANES, LANES)
    copies = jnp.broadcast_to(counts, (ndev, *counts.shape))
    counts_all = lax.all_to_all(copies, "seq", split_axis=0, concat_axis=0, tiled=True)
    counts_all = counts_all.reshape(ndev * counts.shape[0], LANES)

    proj = jnp.dot(token_cond, w_token, preferred_element_type=F32).astype(BF16)
    from_left = shifted(jnp.concatenate([proj, atom_feat[atoms - HALO :]]), 1)
    from_right = shifted(jnp.concatenate([proj, atom_feat[:HALO]]), -1)
    far_left = shifted(proj[tok - HALO :], 2)
    far_right = shifted(proj[:HALO], -2)

    chunks = 3 * tok // LANES
    near = jax.ShapeDtypeStruct((16, LANES), jnp.int32)
    starts, ends, tiles = pl.pallas_call(
        lambda *refs: plan_kernel(*refs, atoms=atoms, pad_chunks=1, chunks=chunks),
        out_shape=(near, near, jax.ShapeDtypeStruct((8, LANES), jnp.int32)),
        scratch_shapes=[pltpu.VMEM((counts_all.shape[0] + 16, LANES), jnp.int32)] * 2,
        name="plan",
    )(counts_all)

    wqkv = jnp.concatenate([w_query, w_key, w_value], axis=1)
    vmem = pl.BlockSpec(memory_space=pltpu.VMEM)
    total = atoms + 2 * PAD
    window = jax.ShapeDtypeStruct((tok, width), BF16)
    atom_out, send_a, send_b, mine = pl.pallas_call(
        lambda *refs: atom_kernel(*refs, atoms=atoms, tok=tok, ndev=ndev),
        in_specs=[pl.BlockSpec(memory_space=pltpu.SMEM)] + [vmem] * 12,
        out_specs=[vmem] * 4,
        out_shape=(
            jax.ShapeDtypeStruct((atoms, width), BF16),
            window,
            window,
            jax.ShapeDtypeStruct((tok, width), F32),
        ),
        scratch_shapes=[
            pltpu.VMEM((3 * tok + 2 * LANES, width), BF16),
            pltpu.VMEM((atoms, 2 * LANES), BF16),
            pltpu.VMEM((total, width), BF16),
            pltpu.VMEM((total, width), BF16),
            pltpu.VMEM((total, width), BF16),
            pltpu.VMEM((total, 2 * width), BF16),
            pltpu.VMEM((atoms, width), BF16),
            pltpu.VMEM((3 * tok + 2 * LANES, width), F32),
        ],
        compiler_params=pltpu.CompilerParams(vmem_limit_bytes=40 << 20),
        name="atoms",
    )(
        tiles, starts, ends, atom_feat, from_left[tok:], from_right[tok:], far_left, from_left[:tok],
        proj, from_right[:tok], far_right, wqkv, w_out,
    )

    got_a = lax.ppermute(send_a, "seq", [(i, i ^ 1) for i in range(ndev)])
    got_b = lax.ppermute(send_b, "seq", [(i, ((i + 1) ^ 1) - 1) for i in range(1, ndev - 1)])
    sums = mine + got_a.astype(F32) + got_b.astype(F32)
    pooled = (sums / atom_counts.astype(F32)[:, None]).astype(BF16)
    token_out = (
        token_cond.astype(F32) + jnp.dot(pooled, w_back, preferred_element_type=F32)
    ).astype(BF16)
    return (token_out, atom_out)


def solution(mesh):
    whole = P()
    rows = P(("batch", "seq"), None)
    in_specs = (rows, rows, P(("batch", "seq")), whole, whole, whole, whole, whole, whole)
    return jax.shard_map(shards, mesh=mesh, in_specs=in_specs, out_specs=(rows, rows), check_vma=False)
```

profile of v0, /device:TPU:136, one launch (start us, length us, event | category | flops | bytes accessed | tf_op | source)
XLA Modules:
  0.0 80.3 jit_solution(2552085200098489535)
XLA Ops:
  0.6 0.0 copy-start
  0.6 0.0 copy-start.8
  0.7 0.0 copy-start.9
  0.7 0.0 copy-start.10
  0.7 1.4 %broadcast_in_dim.4 = s32[16,4,128]{2,1,0:T(4,128)} broadcast(s32[4,128]{1,0:T(4,128)} %bitcast.6), dimensions={1,2} | broadcast | bytes 34816 | tf_op jit(solution)/shard_map/broadcast_in_dim | solution.py:213
  2.0 7.4 %all-to-all-start = ((s32[16,4,128]{2,1,0:T(4,128)}), s32[16,4,128]{2,1,0:T(4,128)S(1)}, u32[]{:S(2)}, u32[]{:S(2)}) async-start(s32[16,4,128]{2,1,0:T(4,128)} %broadcast_in_dim.4), calls=%async_computation | async-start | bytes 65536 | tf_op jit(solution)/shard_map/all_to_all | solution.py:214
  9.4 0.7 fusion.1
  10.1 0.0 copy-start.1
  10.1 0.0 copy-start.2
  10.2 1.6 %convolution_convert_fusion.refs_8_ = bf16[512,128]{1,0:T(8,128)(2,1)S(1)} fusion(bf16[512,768]{1,0:T(8,128)(2,1)} %param.9, bf16[768,128]{1,0:T(8,128)(2,1)} %param.12), kind=kOutput, calls=%fused_computation.1 | convolution fusion | flops 100728832 | bytes 1114112 | tf_op jit(solution)/shard_map/dot_general | solution.py:217
  11.8 2.7 %collective-permute-start.1 = (bf16[560,128]{1,0:T(8,128)(2,1)S(1)}, bf16[560,128]{1,0:T(8,128)(2,1)S(1)}, u32[]{:S(2)}, u32[]{:S(2)}) collective-permute-start(bf16[560,128]{1,0:T(8,128)(2,1)S(1)} %get-tuple-element.20), channel_id=1, source_target_pairs={{0,15},{1,0},{2,1},{3,2},{4,3},{5,4},{6,5},{7,6},{8,7},{9,8},{10,9... | collective-permute-start | bytes 430088 | tf_op jit(solution)/shard_map/ppermute | solution.py:210
  14.6 0.0 collective-permute-start
  14.6 2.3 %collective-permute-start.3 = (bf16[48,128]{1,0:T(8,128)(2,1)S(1)}, bf16[48,128]{1,0:T(8,128)(2,1)S(1)}, u32[]{:S(2)}, u32[]{:S(2)}) collective-permute-start(bf16[48,128]{1,0:T(8,128)(2,1)S(1)} %get-tuple-element.18), channel_id=1, source_target_pairs={{0,14},{1,15},{2,0},{3,1},{4,2},{5,3},{6,4},{7,5},{8,6},{9,7},{10,... | collective-permute-start | bytes 36872 | tf_op jit(solution)/shard_map/ppermute | solution.py:210
  16.9 1.2 %collective-permute-start.2 = (bf16[48,128]{1,0:T(8,128)(2,1)S(1)}, bf16[48,128]{1,0:T(8,128)(2,1)S(1)}, u32[]{:S(2)}, u32[]{:S(2)}) collective-permute-start(bf16[48,128]{1,0:T(8,128)(2,1)S(1)} %get-tuple-element.19), channel_id=1, source_target_pairs={{0,2},{1,3},{2,4},{3,5},{4,6},{5,7},{6,8},{7,9},{8,10},{9,11},{10,... | collective-permute-start | bytes 36872 | tf_op jit(solution)/shard_map/ppermute | solution.py:210
  18.1 0.0 copy-done.8
  18.1 0.0 copy-done.9
  18.1 0.0 copy-done.10
  18.1 0.0 copy-start.6
  18.1 0.0 all-to-all-done
  18.1 0.0 copy-start.7
  18.2 0.6 copy-done.7
  18.8 1.6 %plan.1 = (s32[16,128]{1,0:T(8,128)}, s32[16,128]{1,0:T(8,128)}, s32[8,128]{1,0:T(8,128)}) custom-call(s32[64,128]{1,0:T(8,128)} %bitcast.5), custom_call_target="tpu_custom_call" | custom-call | tf_op jit(solution)/shard_map/plan/pallas_call | solution.py:225
  20.4 0.0 collective-permute-done.1
  20.4 0.0 copy-start.11
  20.4 1.6 %collective-permute-done = bf16[560,128]{1,0:T(8,128)(2,1)S(1)} collective-permute-done((bf16[560,128]{1,0:T(8,128)(2,1)S(1)}, bf16[560,128]{1,0:T(8,128)(2,1)S(1)}, u32[]{:S(2)}, u32[]{:S(2)}) %collective-permute-start) | collective-permute-done | bytes 143392 | tf_op jit(solution)/shard_map/ppermute | solution.py:210
  22.0 0.0 collective-permute-done.3.refs_10_
  22.1 0.9 %collective-permute-done.2.refs_6_ = bf16[48,128]{1,0:T(8,128)(2,1)S(1)} collective-permute-done((bf16[48,128]{1,0:T(8,128)(2,1)S(1)}, bf16[48,128]{1,0:T(8,128)(2,1)S(1)}, u32[]{:S(2)}, u32[]{:S(2)}) %collective-permute-start.2) | collective-permute-done | bytes 12320 | tf_op jit(solution)/shard_map/ppermute | solution.py:210
  23.0 0.0 copy-done.1
  23.0 0.0 copy-done.2
  23.0 0.0 copy-start.3
  23.0 0.7 copy-done.3
  23.7 0.0 copy-start.4
  23.7 0.7 copy-done.4
  24.4 0.0 copy-start.5
  24.4 0.7 copy-done.5
  25.1 42.2 %atoms.1 = (bf16[4096,128]{1,0:T(8,128)(2,1)}, bf16[512,128]{1,0:T(8,128)(2,1)S(1)}, bf16[512,128]{1,0:T(8,128)(2,1)S(1)}, f32[512,128]{1,0:T(8,128)S(1)}) custom-call(s32[8,128]{1,0:T(8,128)S(1)} %copy-done.5, s32[16,128]{1,0:T(8,128)S(1)} %copy-done.3, s32[16,128]{1,0:T(8,128)S(1)} %copy-done.4, bf16[4096,128]{1,0:T(8,128)(2,1)S(1)} %copy-done.1, ...), custom_call_target="tpu_custom_call" | custom-call | tf_op jit(solution)/shard_map/atoms/pallas_call | solution.py:236
  67.3 2.7 %collective-permute-start.4 = (bf16[512,128]{1,0:T(8,128)(2,1)S(1)}, bf16[512,128]{1,0:T(8,128)(2,1)S(1)}, u32[]{:S(2)}, u32[]{:S(2)}) collective-permute-start(bf16[512,128]{1,0:T(8,128)(2,1)S(1)} %get-tuple-element.13), channel_id=1, source_target_pairs={{0,1},{1,0},{2,3},{3,2},{4,5},{5,4},{6,7},{7,6},{8,9},{9,8},{10,11... | collective-permute-start | bytes 393224 | tf_op jit(solution)/shard_map/ppermute | solution.py:263
  70.0 3.6 %collective-permute-start.5 = (bf16[512,128]{1,0:T(8,128)(2,1)S(1)}, bf16[512,128]{1,0:T(8,128)(2,1)S(1)}, u32[]{:S(2)}, u32[]{:S(2)}) collective-permute-start(bf16[512,128]{1,0:T(8,128)(2,1)S(1)} %get-tuple-element.14), channel_id=1, source_target_pairs={{1,2},{2,1},{3,4},{4,3},{5,6},{6,5},{7,8},{8,7},{9,10},{10,9},{11,... | collective-permute-start | bytes 393224 | tf_op jit(solution)/shard_map/ppermute | solution.py:264
  73.6 0.0 copy-done.11
  73.6 0.0 collective-permute-done.4
  73.6 5.3 %collective-permute-done.5 = bf16[512,128]{1,0:T(8,128)(2,1)S(1)} collective-permute-done((bf16[512,128]{1,0:T(8,128)(2,1)S(1)}, bf16[512,128]{1,0:T(8,128)(2,1)S(1)}, u32[]{:S(2)}, u32[]{:S(2)}) %collective-permute-start.5) | collective-permute-done | bytes 131104 | tf_op jit(solution)/shard_map/ppermute | solution.py:264
  78.9 0.0 copy-done
  78.9 0.0 copy-done.6
  78.9 1.3 %add_convert_fusion = bf16[512,768]{1,0:T(8,128)(2,1)} fusion(bf16[512,768]{1,0:T(8,128)(2,1)S(1)} %copy-done.6, bf16[128,768]{1,0:T(8,128)(2,1)S(1)} %copy-done, bf16[512,128]{1,0:T(8,128)(2,1)S(1)} %collective-permute-done.5, f32[512,128]{1,0:T(8,128)S(1)} %get-tuple-element.12, bf16[512,128]{1,0:T(8,128)(2,1)S(1)} %collective-permute-done.4, ...), kind=kOutput, calls=%fused_computation | convolution fusion | flops 102236160 | bytes 2295808 | tf_op jit(solution)/shard_map/dot_general | solution.py:268
  (8 shorter events, 0.1 us)
Async XLA Ops:
  0.6 78.3 %copy-start = (bf16[128,768]{1,0:T(8,128)(2,1)S(1)}, bf16[128,768]{1,0:T(8,128)(2,1)}, u32[]{:S(2)}) copy-start(bf16[128,768]{1,0:T(8,128)(2,1)} %param.17) | copy-start | bytes 589828
  0.6 17.4 %copy-start.8 = (bf16[128,128]{1,0:T(8,128)(2,1)S(1)}, bf16[128,128]{1,0:T(8,128)(2,1)}, u32[]{:S(2)}) copy-start(bf16[128,128]{1,0:T(8,128)(2,1)} %param.15) | copy-start | bytes 98308
  0.7 17.4 %copy-start.9 = (bf16[128,128]{1,0:T(8,128)(2,1)S(1)}, bf16[128,128]{1,0:T(8,128)(2,1)}, u32[]{:S(2)}) copy-start(bf16[128,128]{1,0:T(8,128)(2,1)} %param.14) | copy-start | bytes 98308
  0.7 17.4 %copy-start.10 = (bf16[128,128]{1,0:T(8,128)(2,1)S(1)}, bf16[128,128]{1,0:T(8,128)(2,1)}, u32[]{:S(2)}) copy-start(bf16[128,128]{1,0:T(8,128)(2,1)} %param.13) | copy-start | bytes 98308
  2.0 16.1 %all-to-all-start = ((s32[16,4,128]{2,1,0:T(4,128)}), s32[16,4,128]{2,1,0:T(4,128)S(1)}, u32[]{:S(2)}, u32[]{:S(2)}) async-start(s32[16,4,128]{2,1,0:T(4,128)} %broadcast_in_dim.4), calls=%async_computation | async-start | bytes 65536 | tf_op jit(solution)/shard_map/all_to_all | solution.py:214
  10.1 12.8 %copy-start.1 = (bf16[4096,128]{1,0:T(8,128)(2,1)S(1)}, bf16[4096,128]{1,0:T(8,128)(2,1)}, u32[]{:S(2)}) copy-start(bf16[4096,128]{1,0:T(8,128)(2,1)} %refs_3_.1) | copy-start | bytes 3145732
  10.1 12.8 %copy-start.2 = (bf16[128,128]{1,0:T(8,128)(2,1)S(1)}, bf16[128,128]{1,0:T(8,128)(2,1)}, u32[]{:S(2)}) copy-start(bf16[128,128]{1,0:T(8,128)(2,1)} %refs_12_.1) | copy-start | bytes 98308
  11.8 8.6 %collective-permute-start.1 = (bf16[560,128]{1,0:T(8,128)(2,1)S(1)}, bf16[560,128]{1,0:T(8,128)(2,1)S(1)}, u32[]{:S(2)}, u32[]{:S(2)}) collective-permute-start(bf16[560,128]{1,0:T(8,128)(2,1)S(1)} %get-tuple-element.20), channel_id=1, source_target_pairs={{0,15},{1,0},{2,1},{3,2},{4,3},{5,4},{6,5},{7,6},{8,7},{9,8},{10,9... | collective-permute-start | bytes 430088 | tf_op jit(solution)/shard_map/ppermute | solution.py:210
  14.6 7.5 %collective-permute-start = (bf16[560,128]{1,0:T(8,128)(2,1)S(1)}, bf16[560,128]{1,0:T(8,128)(2,1)S(1)}, u32[]{:S(2)}, u32[]{:S(2)}) collective-permute-start(bf16[560,128]{1,0:T(8,128)(2,1)S(1)} %get-tuple-element.21), channel_id=1, source_target_pairs={{0,1},{1,2},{2,3},{3,4},{4,5},{5,6},{6,7},{7,8},{8,9},{9,10},{10,1... | collective-permute-start | bytes 430088 | tf_op jit(solution)/shard_map/ppermute | solution.py:210
  14.6 7.5 %collective-permute-start.3 = (bf16[48,128]{1,0:T(8,128)(2,1)S(1)}, bf16[48,128]{1,0:T(8,128)(2,1)S(1)}, u32[]{:S(2)}, u32[]{:S(2)}) collective-permute-start(bf16[48,128]{1,0:T(8,128)(2,1)S(1)} %get-tuple-element.18), channel_id=1, source_target_pairs={{0,14},{1,15},{2,0},{3,1},{4,2},{5,3},{6,4},{7,5},{8,6},{9,7},{10,... | collective-permute-start | bytes 36872 | tf_op jit(solution)/shard_map/ppermute | solution.py:210
  16.9 6.1 %collective-permute-start.2 = (bf16[48,128]{1,0:T(8,128)(2,1)S(1)}, bf16[48,128]{1,0:T(8,128)(2,1)S(1)}, u32[]{:S(2)}, u32[]{:S(2)}) collective-permute-start(bf16[48,128]{1,0:T(8,128)(2,1)S(1)} %get-tuple-element.19), channel_id=1, source_target_pairs={{0,2},{1,3},{2,4},{3,5},{4,6},{5,7},{6,8},{7,9},{8,10},{9,11},{10,... | collective-permute-start | bytes 36872 | tf_op jit(solution)/shard_map/ppermute | solution.py:210
  18.1 60.8 %copy-start.6 = (bf16[512,768]{1,0:T(8,128)(2,1)S(1)}, bf16[512,768]{1,0:T(8,128)(2,1)}, u32[]{:S(2)}) copy-start(bf16[512,768]{1,0:T(8,128)(2,1)} %param.9) | copy-start | bytes 2359300
  18.1 0.6 copy-start.7
  20.4 53.2 %copy-start.11 = (s32[512]{0:T(512)S(1)}, s32[512]{0:T(512)}, u32[]{:S(2)}) copy-start(s32[512]{0:T(512)} %param.11) | copy-start | bytes 6148
  23.0 0.7 copy-start.3
  23.7 0.7 copy-start.4
  24.4 0.7 copy-start.5
  67.3 6.3 %collective-permute-start.4 = (bf16[512,128]{1,0:T(8,128)(2,1)S(1)}, bf16[512,128]{1,0:T(8,128)(2,1)S(1)}, u32[]{:S(2)}, u32[]{:S(2)}) collective-permute-start(bf16[512,128]{1,0:T(8,128)(2,1)S(1)} %get-tuple-element.13), channel_id=1, source_target_pairs={{0,1},{1,0},{2,3},{3,2},{4,5},{5,4},{6,7},{7,6},{8,9},{9,8},{10,11... | collective-permute-start | bytes 393224 | tf_op jit(solution)/shard_map/ppermute | solution.py:263
  70.0 9.0 %collective-permute-start.5 = (bf16[512,128]{1,0:T(8,128)(2,1)S(1)}, bf16[512,128]{1,0:T(8,128)(2,1)S(1)}, u32[]{:S(2)}, u32[]{:S(2)}) collective-permute-start(bf16[512,128]{1,0:T(8,128)(2,1)S(1)} %get-tuple-element.14), channel_id=1, source_target_pairs={{1,2},{2,1},{3,4},{4,3},{5,6},{6,5},{7,8},{8,7},{9,10},{10,9},{11,... | collective-permute-start | bytes 393224 | tf_op jit(solution)/shard_map/ppermute | solution.py:264
where the time goes:
time: 81.8 us; the launch traced here: 80.3 us
  Pallas kernels  43.9 us (54%)
  starting transfers between devices  19.9 us (24%)
  waiting for transfers between devices  7.85 us (10%)
  local copies, waits for them, and re-layouts  4.82 us (6%)
  matrix products  2.93 us (4%)
    pallas_call x1, Pallas kernels, shards(): pl.pallas_call(lambda *refs: atom_kernel(*refs, atoms=atoms, tok=tok, nde...  42.2 us
    all_to_all x1, starting transfers between devices, shards(): lax.all_to_all(copies, 'seq', split_axis=0, concat_axis=0, tiled=True)  7.39 us
    ppermute x4, starting transfers between devices, shifted(): return lax.ppermute(x, 'seq', [(i, (i + by) % ndev) for i in range(ndev)])  6.28 us
    ppermute x1, waiting for transfers between devices, shards(): lax.ppermute(send_b, 'seq', [(i, (i + 1 ^ 1) - 1) for i in range(1, ndev...  5.32 us
    ppermute x1, starting transfers between devices, shards(): lax.ppermute(send_b, 'seq', [(i, (i + 1 ^ 1) - 1) for i in range(1, ndev...  3.6 us
    unnamed x24, local copies, waits for them, and re-layouts  2.72 us
    ppermute x1, starting transfers between devices, shards(): got_a = lax.ppermute(send_a, 'seq', [(i, i ^ 1) for i in range(ndev)])  2.67 us
    ppermute x4, waiting for transfers between devices, shifted(): return lax.ppermute(x, 'seq', [(i, (i + by) % ndev) for i in range(ndev)])  2.52 us
  transfers between devices with their start and end apart: 7, of which 3 were waited for; matrix products, arithmetic and copies ran while one was open for 3% of the time, Pallas kernels for 2%

commit v1 on v0

v1 whole, which is shorter than its diff:
```python
import math

import jax
import jax.numpy as jnp
from jax import lax
from jax.experimental import pallas as pl
from jax.experimental.pallas import tpu as pltpu
from jax.sharding import PartitionSpec as P

BF16 = jnp.bfloat16
F32 = jnp.float32
HEADS = 4
QBLOCK = 32
KEYS = 128
HALO = 48
LANES = 128
ONES = 16
PAD = 64
NT = (((1,), (1,)), ((), ()))
TN = (((0,), (0,)), ((), ()))


def plan_kernel(counts_ref, near_ref, far_ref, spad, epad, *, atoms, pad_chunks, chunks):
    position = lax.axis_index("seq")
    rows = counts_ref.shape[0]
    counts = counts_ref[...].astype(F32)
    exact = counts.astype(BF16)
    up_to = (
        lax.broadcasted_iota(jnp.int32, (LANES, LANES), 0)
        <= lax.broadcasted_iota(jnp.int32, (LANES, LANES), 1)
    )
    within = jnp.dot(exact, up_to.astype(F32).astype(BF16), preferred_element_type=F32)
    before = (
        lax.broadcasted_iota(jnp.int32, (rows, rows), 1)
        < lax.broadcasted_iota(jnp.int32, (rows, rows), 0)
    )
    ahead = jnp.dot(before.astype(F32).astype(BF16), exact, preferred_element_type=F32)
    ends = (within + jnp.sum(ahead, axis=1, keepdims=True)).astype(jnp.int32) - position * atoms
    row = lax.broadcasted_iota(jnp.int32, (rows, LANES), 0) + 1
    lane = lax.broadcasted_iota(jnp.int32, (rows, LANES), 1)
    per_dev = chunks // 3
    drift = ends + position * atoms - row // per_dev * atoms
    closes = (row % per_dev == 0) & (lane == LANES - 1)
    wide = jnp.where(closes & (jnp.abs(drift) > atoms - HALO), 1.0, 0.0)
    far_ref[0, 0] = jnp.max(wide).astype(jnp.int32)
    far = 1 << 24
    spad[0:8, :] = jnp.full((8, LANES), -far, jnp.int32)
    epad[0:8, :] = jnp.full((8, LANES), -far, jnp.int32)
    spad[8 + rows : 16 + rows, :] = jnp.full((8, LANES), far, jnp.int32)
    epad[8 + rows : 16 + rows, :] = jnp.full((8, LANES), far, jnp.int32)
    spad[8 : 8 + rows, :] = ends - counts_ref[...]
    epad[8 : 8 + rows, :] = ends
    first = position * (chunks // 3) - (chunks // 3) - pad_chunks + 8
    near_ends = epad[pl.ds(first, 16), :]
    near_ref[8:24, :] = spad[pl.ds(first, 16), :]
    near_ref[24:, :] = near_ends
    lane = lax.broadcasted_iota(jnp.int32, (16, LANES), 1)
    row = lax.broadcasted_iota(jnp.int32, (16, LANES), 0)
    tiles = atoms // LANES
    tile_start = jnp.where(lane == tiles, -HALO, lane * LANES)
    tile_start = jnp.where(lane == tiles + 1, atoms, tile_start)
    total = chunks + 2 * pad_chunks
    passed = (near_ends[:, LANES - 1 :] <= tile_start) & (row < total)
    index = jnp.sum(passed.astype(F32), axis=0, keepdims=True).astype(jnp.int32)
    index = jnp.minimum(index, total - 2)
    near_ref[:8, :] = jnp.broadcast_to(index, (8, LANES))


def atom_kernel(
    tiles_ref, near_ref, feat_ref, left_ref, own_ref, right_ref, far_ref,
    wq_ref, wk_ref, wv_ref, wout_ref,
    out_ref, send_a_ref, send_b_ref, mine_ref,
    table, member, xs, qx, ks, vs, os, acc,
    *, atoms, tok, ndev,
):
    position = lax.axis_index("seq")
    tiles = atoms // LANES
    edge = far_ref.shape[0] // 2
    zero = jnp.zeros((LANES - edge, LANES), BF16)
    base = LANES
    table[0 : base - edge, :] = zero
    table[base - edge : base, :] = far_ref[:edge, :]
    table[base : base + tok, :] = left_ref[:tok, :]
    table[base + tok : base + 2 * tok, :] = own_ref[...]
    table[base + 2 * tok : base + 3 * tok, :] = right_ref[:tok, :]
    table[base + 3 * tok : base + 3 * tok + edge, :] = far_ref[edge:, :]
    table[base + 3 * tok + edge :, :] = zero

    def members(chunk, first, height):
        ids = lax.broadcasted_iota(jnp.int32, (height, 2 * LANES), 0)
        lo = jnp.concatenate([near_ref[pl.ds(chunk + 8, 1), :], near_ref[pl.ds(chunk + 9, 1), :]], axis=1) - first
        hi = jnp.concatenate([near_ref[pl.ds(chunk + 24, 1), :], near_ref[pl.ds(chunk + 25, 1), :]], axis=1) - first
        return jnp.where((ids >= lo) & (ids < hi), 1.0, 0.0).astype(BF16)

    def rows_of(chunk, hit):
        window = table[pl.ds(pl.multiple_of(chunk * LANES, LANES), 2 * LANES), :]
        return jnp.dot(hit, window, preferred_element_type=F32)

    def halo_rows(index, first, feat):
        chunk = tiles_ref[0, index]
        got = rows_of(chunk, members(chunk, first, HALO))
        return (feat.astype(F32) + got).astype(BF16)

    xs[0 : PAD - HALO, :] = jnp.zeros((PAD - HALO, LANES), BF16)
    xs[PAD + atoms + HALO :, :] = jnp.zeros((PAD - HALO, LANES), BF16)
    xs[PAD - HALO : PAD, :] = halo_rows(tiles, -HALO, left_ref[tok + PAD - HALO :, :])
    xs[PAD + atoms : PAD + atoms + HALO, :] = halo_rows(tiles + 1, atoms, right_ref[tok : tok + HALO, :])

    group = 16
    pgroup = 16

    def gather(i, carry):
        for j in range(group):
            t = i * group + j
            at = pl.multiple_of(t * LANES, LANES)
            chunk = tiles_ref[0, t]
            hit = members(chunk, at, LANES)
            member[pl.ds(at, LANES), :] = hit
            x = feat_ref[pl.ds(at, LANES), :].astype(F32) + rows_of(chunk, hit)
            xs[pl.ds(at + PAD, LANES), :] = x.astype(BF16)
        return carry

    lax.fori_loop(0, tiles // group, gather, 0)

    steps = 1
    span = (atoms + 2 * PAD) // steps
    broad = 4096
    wqt = wq_ref[...].T
    wvt = wv_ref[...].T

    def project(i, carry):
        at = pl.multiple_of(i * span, LANES)
        x = xs[pl.ds(at, span), :]
        ks[pl.ds(at, span), :] = jnp.dot(x, wk_ref[...], preferred_element_type=F32).astype(BF16)
        r = lax.dot_general(wvt, x, NT, preferred_element_type=F32).astype(BF16)
        vs[:LANES, pl.ds(at, span)] = r
        vs[LANES:, pl.ds(at, span)] = jnp.ones((ONES, span), BF16)
        return carry

    def turned(x, h):
        return pltpu.roll(x, h * QBLOCK % LANES, 1) if h % HEADS else x

    def ask(i, carry):
        at = pl.multiple_of(i * broad, LANES)
        r = lax.dot_general(wqt, xs[pl.ds(at + PAD, broad), :], NT, preferred_element_type=F32).astype(BF16)
        for c in range(broad // LANES):
            for h in range(HEADS):
                part = r[h * QBLOCK : (h + 1) * QBLOCK, c * LANES : (c + 1) * LANES]
                qx[h * QBLOCK : (h + 1) * QBLOCK, pl.ds(at + c * LANES, LANES)] = turned(part, h)
        return carry

    lax.fori_loop(0, steps, project, 0)
    lax.fori_loop(0, atoms // broad, ask, 0)

    lane = lax.broadcasted_iota(jnp.int32, vs.shape[:1] + (LANES,), 1)

    @pl.when(position == 0)
    def _():
        ks[PAD - HALO : PAD, :] = jnp.broadcast_to(ks[PAD : PAD + 1, :].astype(F32), (HALO, LANES)).astype(BF16)
        vs[:, :LANES] = jnp.where(lane < PAD, 0.0, vs[:, :LANES].astype(F32)).astype(BF16)

    @pl.when(position == ndev - 1)
    def _():
        last = PAD + atoms
        ks[last : last + HALO, :] = jnp.broadcast_to(ks[last - 1 : last, :].astype(F32), (HALO, LANES)).astype(BF16)
        vs[:, atoms:] = jnp.where(lane >= PAD, 0.0, vs[:, atoms:].astype(F32)).astype(BF16)

    head = LANES // HEADS
    scale = math.log2(math.e) / math.sqrt(head)
    row_group = lax.broadcasted_iota(jnp.int32, (LANES, LANES), 0) // head
    lane_group = lax.broadcasted_iota(jnp.int32, (LANES, LANES), 1) // QBLOCK
    kept = [((row_group + j) % HEADS == lane_group).astype(F32).astype(BF16) for j in range(4)]
    group_of = lax.broadcasted_iota(jnp.int32, (head, LANES), 1) // QBLOCK
    blank = jnp.zeros((LANES, LANES), BF16)

    per = 4

    def attend(i, carry):
        for n in range(per):
            at = pl.multiple_of((i * per + n) * LANES, LANES)
            q = qx[:, pl.ds(at, LANES)]
            value = vs[:, pl.ds(at, 2 * LANES)]
            parts = []
            for j in (0, 2):
                key = [ks[pl.ds(at + PAD - HALO + (j + c) * QBLOCK, KEYS), :] for c in range(2)]
                ask_for = jnp.concatenate(
                    [
                        jnp.concatenate([q * kept[j], blank], axis=1),
                        jnp.concatenate([blank, q * kept[j + 1]], axis=1),
                    ],
                    axis=0,
                )
                s = jnp.dot(jnp.concatenate(key, axis=1), ask_for, preferred_element_type=F32)
                top = jnp.max(s, axis=0, keepdims=True)
                p = jnp.exp2((s - top) * scale).astype(BF16)
                cols = []
                for c in range(2):
                    above = PAD - HALO + (j + c) * QBLOCK
                    cols.append(
                        jnp.concatenate(
                            [
                                jnp.zeros((above, LANES), BF16),
                                p[:, c * LANES : (c + 1) * LANES],
                                jnp.zeros((LANES - above, LANES), BF16),
                            ],
                            axis=0,
                        )
                    )
                o = jnp.dot(value, jnp.concatenate(cols, axis=1), preferred_element_type=F32)
                parts += [o[:, :LANES], o[:, LANES:]]
            for h in range(HEADS):
                o = parts[0][h * head : (h + 1) * head, :]
                total = parts[0][LANES : LANES + 1, :]
                for j in range(1, 4):
                    here = group_of == (h + j) % HEADS
                    o = jnp.where(here, parts[j][h * head : (h + 1) * head, :], o)
                    total = jnp.where(here[:1], parts[j][LANES : LANES + 1, :], total)
                o = (o * (1.0 / total)).astype(BF16)
                os[h * head : (h + 1) * head, pl.ds(at, LANES)] = turned(o, -h % HEADS)
        return carry

    lax.fori_loop(0, atoms // LANES // per, attend, 0)

    tall = 4096

    def finish(i, carry):
        at = pl.multiple_of(i * tall, tall)
        r = lax.dot_general(os[:, pl.ds(at, tall)], wout_ref[...], TN, preferred_element_type=F32)
        out_ref[pl.ds(at, tall), :] = (xs[pl.ds(at + PAD, tall), :].astype(F32) + r).astype(BF16)
        return carry

    lax.fori_loop(0, atoms // tall, finish, 0)

    acc[...] = jnp.zeros_like(acc)

    def pool(i, carry):
        for j in range(pgroup):
            t = i * pgroup + j
            at = pl.multiple_of(t * LANES, LANES)
            chunk = tiles_ref[0, t]
            part = lax.dot_general(
                out_ref[pl.ds(at, LANES), :], member[pl.ds(at, LANES), :], TN, preferred_element_type=F32
            )
            to = pl.ds(pl.multiple_of(chunk * LANES, LANES), 2 * LANES)
            acc[:, to] = acc[:, to] + part
        return carry

    lax.fori_loop(0, tiles // pgroup, pool, 0)
    odd = lax.rem(position, 2)
    from_a = pl.multiple_of(base + (1 - odd) * 2 * tok, LANES)
    from_b = pl.multiple_of(base + odd * 2 * tok, LANES)
    send_a_ref[...] = acc[:, pl.ds(from_a, tok)].astype(BF16)
    send_b_ref[...] = acc[:, pl.ds(from_b, tok)].astype(BF16)
    mine_ref[...] = acc[:, base + tok : base + 2 * tok]


def shards(token_cond, atom_feat, atom_counts, w_token, w_query, w_key, w_value, w_out, w_back):
    tok = token_cond.shape[0]
    atoms, width = atom_feat.shape
    ndev = lax.axis_size("seq")

    def shifted(x, by):
        return lax.ppermute(x, "seq", [(i, (i + by) % ndev) for i in range(ndev)])

    counts = atom_counts.reshape(tok // LANES, LANES)
    copies = jnp.broadcast_to(counts, (ndev, *counts.shape))
    counts_all = lax.all_to_all(copies, "seq", split_axis=0, concat_axis=0, tiled=True)
    counts_all = counts_all.reshape(ndev * counts.shape[0], LANES)

    proj = jnp.dot(token_cond, w_token, preferred_element_type=F32).astype(BF16)
    from_left = shifted(jnp.concatenate([proj, atom_feat[atoms - PAD :]]), 1)
    from_right = shifted(jnp.concatenate([proj, atom_feat[:PAD]]), -1)
    whole = pl.BlockSpec(memory_space=pltpu.VMEM)

    chunks = 3 * tok // LANES
    near, far = pl.pallas_call(
        lambda *refs: plan_kernel(*refs, atoms=atoms, pad_chunks=1, chunks=chunks),
        out_shape=(
            jax.ShapeDtypeStruct((40, LANES), jnp.int32),
            jax.ShapeDtypeStruct((1, 1), jnp.int32),
        ),
        in_specs=[whole],
        out_specs=[whole] + [pl.BlockSpec(memory_space=pltpu.SMEM)],
        scratch_shapes=[pltpu.VMEM((counts_all.shape[0] + 16, LANES), jnp.int32)] * 2,
        name="plan",
    )(counts_all)

    beyond = lax.cond(
        far[0, 0] > 0,
        lambda x: jnp.concatenate([shifted(x[tok - HALO :], 2), shifted(x[:HALO], -2)]),
        lambda x: jnp.zeros((2 * HALO, width), BF16),
        proj,
    )
    vmem = whole
    total = atoms + 2 * PAD
    window = jax.ShapeDtypeStruct((width, tok), BF16)
    atom_out, send_a, send_b, mine = pl.pallas_call(
        lambda *refs: atom_kernel(*refs, atoms=atoms, tok=tok, ndev=ndev),
        in_specs=[pl.BlockSpec(memory_space=pltpu.SMEM)] + [vmem] * 10,
        out_specs=[vmem] * 4,
        out_shape=(
            jax.ShapeDtypeStruct((atoms, width), BF16),
            window,
            window,
            jax.ShapeDtypeStruct((width, tok), F32),
        ),
        scratch_shapes=[
            pltpu.VMEM((3 * tok + 2 * LANES, width), BF16),
            pltpu.VMEM((atoms, 2 * LANES), BF16),
            pltpu.VMEM((total, width), BF16),
            pltpu.VMEM((width, atoms), BF16),
            pltpu.VMEM((total, width), BF16),
            pltpu.VMEM((width + ONES, total), BF16),
            pltpu.VMEM((width, atoms), BF16),
            pltpu.VMEM((width, 3 * tok + 2 * LANES), F32),
        ],
        compiler_params=pltpu.CompilerParams(vmem_limit_bytes=40 << 20),
        name="atoms",
    )(
        near, near, atom_feat, from_left, proj, from_right, beyond, w_query, w_key, w_value, w_out,
    )

    got_a = lax.ppermute(send_a, "seq", [(i, i ^ 1) for i in range(ndev)])
    got_b = lax.ppermute(send_b, "seq", [(i, ((i + 1) ^ 1) - 1) for i in range(1, ndev - 1)])
    sums = mine + got_a.astype(F32) + got_b.astype(F32)
    pooled = (sums / atom_counts.astype(F32)[None, :]).astype(BF16)
    token_out = (
        token_cond.astype(F32) + lax.dot_general(pooled, w_back, TN, preferred_element_type=F32)
    ).astype(BF16)
    return (token_out, atom_out)


def solution(mesh):
    whole = P()
    rows = P(("batch", "seq"), None)
    in_specs = (rows, rows, P(("batch", "seq")), whole, whole, whole, whole, whole, whole)
    return jax.shard_map(shards, mesh=mesh, in_specs=in_specs, out_specs=(rows, rows), check_vma=False)
```

time: 81.8 us -> 50.6 us (0.62); the launches traced: 80.3 us -> 50.3 us
  Pallas kernels: 43.9 us -> 15 us
  waiting for transfers between devices: 7.85 us -> 11.1 us
  starting transfers between devices: 19.9 us -> 17 us
  local copies, waits for them, and re-layouts: 4.82 us -> 2.83 us
    pallas_call x1, Pallas kernels: 42.2 us -> 13.3 us  [shards(): pl.pallas_call(lambda *refs: atom_kernel(*refs, atoms=atoms, tok=tok, nde...]
    all_to_all x1, waiting for transfers between devices: 0.01 us -> 6.24 us  [shards(): lax.all_to_all(copies, 'seq', split_axis=0, concat_axis=0, tiled=True)]
    ppermute x4 -> x2, starting transfers between devices: 6.28 us -> 2.72 us  [shifted(): return lax.ppermute(x, 'seq', [(i, (i + by) % ndev) for i in range(ndev)])]
    ppermute x4 -> x2, waiting for transfers between devices: 2.52 us -> 0.01 us  [shifted(): return lax.ppermute(x, 'seq', [(i, (i + by) % ndev) for i in range(ndev)])]
    all_to_all x1, starting transfers between devices: 7.39 us -> 9.65 us  [shards(): lax.all_to_all(copies, 'seq', split_axis=0, concat_axis=0, tiled=True)]
    ppermute x1, starting transfers between devices: 2.67 us -> 0.57 us  [shards(): got_a = lax.ppermute(send_a, 'seq', [(i, i ^ 1) for i in range(ndev)])]
    unnamed x24 -> x20, local copies, waits for them, and re-layouts: 2.72 us -> 1.38 us
  transfers between devices with their start and end apart: 7 -> 5, of which waited for: 3 -> 3; matrix products, arithmetic and copies ran while one was open for 3% -> 1% of each run, Pallas kernels for 2% -> 3%
where the time goes in v1:
time: 50.6 us; the launch traced here: 50.3 us
  starting transfers between devices  17 us (34%)
  Pallas kernels  15 us (30%)
  waiting for transfers between devices  11.1 us (22%)
  local copies, waits for them, and re-layouts  2.83 us (6%)
  matrix products  2.82 us (6%)
  between operations  1.43 us (3%)
    pallas_call x1, Pallas kernels, shards(): pl.pallas_call(lambda *refs: atom_kernel(*refs, atoms=atoms, tok=tok, nde...  13.3 us
    all_to_all x1, starting transfers between devices, shards(): lax.all_to_all(copies, 'seq', split_axis=0, concat_axis=0, tiled=True)  9.65 us
    all_to_all x1, waiting for transfers between devices, shards(): lax.all_to_all(copies, 'seq', split_axis=0, concat_axis=0, tiled=True)  6.24 us
    ppermute x1, waiting for transfers between devices, shards(): lax.ppermute(send_b, 'seq', [(i, (i + 1 ^ 1) - 1) for i in range(1, ndev...  4.56 us
    ppermute x1, starting transfers between devices, shards(): lax.ppermute(send_b, 'seq', [(i, (i + 1 ^ 1) - 1) for i in range(1, ndev...  4.04 us
    ppermute x2, starting transfers between devices, shifted(): return lax.ppermute(x, 'seq', [(i, (i + by) % ndev) for i in range(ndev)])  2.72 us
    pallas_call x1, Pallas kernels, shards(): pl.pallas_call(lambda *refs: plan_kernel(*refs, atoms=atoms, pad_chunks=1...  1.68 us
    dot_general x1, matrix products, shards(): proj = jnp.dot(token_cond, w_token, preferred_element_type=F32).astype(BF16)  1.53 us
  transfers between devices with their start and end apart: 5, of which 3 were waited for; matrix products, arithmetic and copies ran while one was open for 1% of the time, Pallas kernels for 3%

profile of v1, /device:TPU:136, one launch (start us, length us, event | category | flops | bytes accessed | tf_op | source)
XLA Modules:
  0.0 50.3 jit_solution(3467264500468099506)
XLA Ops:
  0.6 0.0 copy-start
  0.6 0.0 copy-start.1
  0.7 0.0 copy-start.9
  0.7 0.0 copy-start.6
  0.7 0.0 copy-start.5
  0.7 0.0 copy-start.4
  0.7 0.0 copy-start.3
  0.7 0.8 %fusion.2 = (bf16[64,128]{1,0:T(8,128)(2,1)S(1)}, bf16[64,128]{1,0:T(8,128)(2,1)S(1)}) fusion(bf16[4096,128]{1,0:T(8,128)(2,1)} %refs_2_.1), kind=kLoop, calls=%fused_computation.8 | loop fusion | bytes 65536 | tf_op jit(solution)/shard_map/slice | solution.py:272
  1.5 1.5 %convolution_convert_fusion.refs_4_ = bf16[512,128]{1,0:T(8,128)(2,1)S(1)} fusion(bf16[512,768]{1,0:T(8,128)(2,1)} %param.11, bf16[768,128]{1,0:T(8,128)(2,1)} %param.14), kind=kOutput, calls=%fused_computation.2 | convolution fusion | flops 100728832 | bytes 1114112 | tf_op jit(solution)/shard_map/dot_general | solution.py:270
  3.1 2.7 %collective-permute-start.3 = (bf16[576,128]{1,0:T(8,128)(2,1)S(1)}, bf16[576,128]{1,0:T(8,128)(2,1)S(1)}, u32[]{:S(2)}, u32[]{:S(2)}) collective-permute-start(bf16[576,128]{1,0:T(8,128)(2,1)S(1)} %get-tuple-element.22), channel_id=1, source_target_pairs={{0,15},{1,0},{2,1},{3,2},{4,3},{5,4},{6,5},{7,6},{8,7},{9,8},{10,9... | collective-permute-start | bytes 442376 | tf_op jit(solution)/shard_map/ppermute | solution.py:263
  5.8 0.0 collective-permute-start.2
  5.8 0.0 copy-done.9
  5.8 0.6 %broadcast_in_dim.4 = s32[16,4,128]{2,1,0:T(4,128)} broadcast(s32[4,128]{1,0:T(4,128)S(1)} %bitcast.7), dimensions={1,2} | broadcast | bytes 34816 | tf_op jit(solution)/shard_map/broadcast_in_dim | solution.py:266
  6.5 9.6 %all-to-all-start = ((s32[16,4,128]{2,1,0:T(4,128)}), s32[16,4,128]{2,1,0:T(4,128)S(1)}, u32[]{:S(2)}, u32[]{:S(2)}) async-start(s32[16,4,128]{2,1,0:T(4,128)} %broadcast_in_dim.4), calls=%async_computation | async-start | bytes 65536 | tf_op jit(solution)/shard_map/all_to_all | solution.py:267
  16.1 6.2 %all-to-all-done = s32[16,4,128]{2,1,0:T(4,128)S(1)} async-done(((s32[16,4,128]{2,1,0:T(4,128)}), s32[16,4,128]{2,1,0:T(4,128)S(1)}, u32[]{:S(2)}, u32[]{:S(2)}) %all-to-all-start) | async-done | bytes 32800 | tf_op jit(solution)/shard_map/all_to_all | solution.py:267
  22.3 0.0 copy-start.8
  22.3 0.6 %copy-done.8 = s32[16,4,128]{2,1,0:T(4,128)} copy-done((s32[16,4,128]{2,1,0:T(4,128)}, s32[16,4,128]{2,1,0:T(4,128)S(1)}, u32[]{:S(2)}) %copy-start.8) | copy-done | bytes 32792
  23.0 1.7 %plan.1 = (s32[40,128]{1,0:T(8,128)}, s32[1,1]{1,0:T(1,128)}) custom-call(s32[64,128]{1,0:T(8,128)} %bitcast.6), custom_call_target="tpu_custom_call" | custom-call | tf_op jit(solution)/shard_map/plan/pallas_call | solution.py:276
  25.3 0.0 collective-permute-done.3.refs_5_
  25.3 0.0 collective-permute-done.2.refs_3_
  25.3 0.0 copy-done.1
  25.3 0.0 copy-done.6
  25.3 0.0 copy-done.5
  25.3 0.0 copy-done.4
  25.4 0.0 copy-done.3
  25.4 0.0 copy-start.2
  25.4 0.7 %copy-done.2 = s32[40,128]{1,0:T(8,128)S(1)} copy-done((s32[40,128]{1,0:T(8,128)S(1)}, s32[40,128]{1,0:T(8,128)}, u32[]{:S(2)}) %copy-start.2) | copy-done | bytes 20504
  26.1 0.0 copy-start.7
  26.1 13.3 %atoms.1 = (bf16[4096,128]{1,0:T(8,128)(2,1)}, bf16[128,512]{1,0:T(8,128)(2,1)S(1)}, bf16[128,512]{1,0:T(8,128)(2,1)S(1)}, f32[128,512]{1,0:T(8,128)S(1)}) custom-call(s32[40,128]{1,0:T(8,128)S(1)} %copy-done.2, s32[40,128]{1,0:T(8,128)S(1)} %copy-done.2, bf16[4096,128]{1,0:T(8,128)(2,1)S(1)} %copy-done.1, ...), custom_call_target="tpu_custom_call" | custom-call | tf_op jit(solution)/shard_map/atoms/pallas_call | solution.py:297
  39.4 0.6 %collective-permute-start.4 = (bf16[128,512]{1,0:T(8,128)(2,1)S(1)}, bf16[128,512]{1,0:T(8,128)(2,1)S(1)}, u32[]{:S(2)}, u32[]{:S(2)}) collective-permute-start(bf16[128,512]{1,0:T(8,128)(2,1)S(1)} %get-tuple-element.15), channel_id=1, source_target_pairs={{0,1},{1,0},{2,3},{3,2},{4,5},{5,4},{6,7},{7,6},{8,9},{9,8},{10,11... | collective-permute-start | bytes 393224 | tf_op jit(solution)/shard_map/ppermute | solution.py:323
  40.0 4.0 %collective-permute-start.5 = (bf16[128,512]{1,0:T(8,128)(2,1)S(1)}, bf16[128,512]{1,0:T(8,128)(2,1)S(1)}, u32[]{:S(2)}, u32[]{:S(2)}) collective-permute-start(bf16[128,512]{1,0:T(8,128)(2,1)S(1)} %get-tuple-element.16), channel_id=1, source_target_pairs={{1,2},{2,1},{3,4},{4,3},{5,6},{6,5},{7,8},{8,7},{9,10},{10,9},{11,... | collective-permute-start | bytes 393224 | tf_op jit(solution)/shard_map/ppermute | solution.py:324
  44.1 0.3 collective-permute-done.4
  44.4 4.6 %collective-permute-done.5 = bf16[128,512]{1,0:T(8,128)(2,1)S(1)} collective-permute-done((bf16[128,512]{1,0:T(8,128)(2,1)S(1)}, bf16[128,512]{1,0:T(8,128)(2,1)S(1)}, u32[]{:S(2)}, u32[]{:S(2)}) %collective-permute-start.5) | collective-permute-done | bytes 131104 | tf_op jit(solution)/shard_map/ppermute | solution.py:324
  49.0 0.0 copy-done
  49.0 0.0 copy-done.7
  49.0 1.3 %add_convert_fusion = bf16[512,768]{1,0:T(8,128)(2,1)} fusion(bf16[512,768]{1,0:T(8,128)(2,1)S(1)} %copy-done.7, bf16[128,768]{1,0:T(8,128)(2,1)S(1)} %copy-done, bf16[128,512]{1,0:T(8,128)(2,1)S(1)} %collective-permute-done.5, f32[128,512]{1,0:T(8,128)S(1)} %get-tuple-element.14, bf16[128,512]{1,0:T(8,128)(2,1)S(1)} %collective-permute-done.4, ...), kind=kOutput, calls=%fused_computation.1 | convolution fusion | flops 102236160 | bytes 2295808 | tf_op jit(solution)/shard_map/dot_general | solution.py:328
  (4 shorter events, 0.1 us)
Async XLA Ops:
  0.6 48.3 %copy-start = (bf16[128,768]{1,0:T(8,128)(2,1)S(1)}, bf16[128,768]{1,0:T(8,128)(2,1)}, u32[]{:S(2)}) copy-start(bf16[128,768]{1,0:T(8,128)(2,1)} %param.19) | copy-start | bytes 589828
  0.6 24.7 %copy-start.1 = (bf16[4096,128]{1,0:T(8,128)(2,1)S(1)}, bf16[4096,128]{1,0:T(8,128)(2,1)}, u32[]{:S(2)}) copy-start(bf16[4096,128]{1,0:T(8,128)(2,1)} %refs_2_.1) | copy-start | bytes 3145732
  0.7 5.2 %copy-start.9 = (s32[512]{0:T(512)S(1)}, s32[512]{0:T(512)}, u32[]{:S(2)}) copy-start(s32[512]{0:T(512)} %param.13) | copy-start | bytes 6148
  0.7 24.7 %copy-start.6 = (bf16[128,128]{1,0:T(8,128)(2,1)S(1)}, bf16[128,128]{1,0:T(8,128)(2,1)}, u32[]{:S(2)}) copy-start(bf16[128,128]{1,0:T(8,128)(2,1)} %refs_10_.1) | copy-start | bytes 98308
  0.7 24.7 %copy-start.5 = (bf16[128,128]{1,0:T(8,128)(2,1)S(1)}, bf16[128,128]{1,0:T(8,128)(2,1)}, u32[]{:S(2)}) copy-start(bf16[128,128]{1,0:T(8,128)(2,1)} %refs_9_.1) | copy-start | bytes 98308
  0.7 24.7 %copy-start.4 = (bf16[128,128]{1,0:T(8,128)(2,1)S(1)}, bf16[128,128]{1,0:T(8,128)(2,1)}, u32[]{:S(2)}) copy-start(bf16[128,128]{1,0:T(8,128)(2,1)} %refs_8_.1) | copy-start | bytes 98308
  0.7 24.7 %copy-start.3 = (bf16[128,128]{1,0:T(8,128)(2,1)S(1)}, bf16[128,128]{1,0:T(8,128)(2,1)}, u32[]{:S(2)}) copy-start(bf16[128,128]{1,0:T(8,128)(2,1)} %refs_7_.1) | copy-start | bytes 98308
  3.1 22.2 %collective-permute-start.3 = (bf16[576,128]{1,0:T(8,128)(2,1)S(1)}, bf16[576,128]{1,0:T(8,128)(2,1)S(1)}, u32[]{:S(2)}, u32[]{:S(2)}) collective-permute-start(bf16[576,128]{1,0:T(8,128)(2,1)S(1)} %get-tuple-element.22), channel_id=1, source_target_pairs={{0,15},{1,0},{2,1},{3,2},{4,3},{5,4},{6,5},{7,6},{8,7},{9,8},{10,9... | collective-permute-start | bytes 442376 | tf_op jit(solution)/shard_map/ppermute | solution.py:263
  5.8 19.5 %collective-permute-start.2 = (bf16[576,128]{1,0:T(8,128)(2,1)S(1)}, bf16[576,128]{1,0:T(8,128)(2,1)S(1)}, u32[]{:S(2)}, u32[]{:S(2)}) collective-permute-start(bf16[576,128]{1,0:T(8,128)(2,1)S(1)} %get-tuple-element.23), channel_id=1, source_target_pairs={{0,1},{1,2},{2,3},{3,4},{4,5},{5,6},{6,7},{7,8},{8,9},{9,10},{10,1... | collective-permute-start | bytes 442376 | tf_op jit(solution)/shard_map/ppermute | solution.py:263
  6.5 15.9 %all-to-all-start = ((s32[16,4,128]{2,1,0:T(4,128)}), s32[16,4,128]{2,1,0:T(4,128)S(1)}, u32[]{:S(2)}, u32[]{:S(2)}) async-start(s32[16,4,128]{2,1,0:T(4,128)} %broadcast_in_dim.4), calls=%async_computation | async-start | bytes 65536 | tf_op jit(solution)/shard_map/all_to_all | solution.py:267
  22.3 0.6 %copy-start.8 = (s32[16,4,128]{2,1,0:T(4,128)}, s32[16,4,128]{2,1,0:T(4,128)S(1)}, u32[]{:S(2)}) copy-start(s32[16,4,128]{2,1,0:T(4,128)S(1)} %all-to-all-done) | copy-start | bytes 98308
  25.4 0.7 %copy-start.2 = (s32[40,128]{1,0:T(8,128)S(1)}, s32[40,128]{1,0:T(8,128)}, u32[]{:S(2)}) copy-start(s32[40,128]{1,0:T(8,128)} %get-tuple-element.12.refs_0_.refs_1_) | copy-start | bytes 61444
  26.1 22.9 %copy-start.7 = (bf16[512,768]{1,0:T(8,128)(2,1)S(1)}, bf16[512,768]{1,0:T(8,128)(2,1)}, u32[]{:S(2)}) copy-start(bf16[512,768]{1,0:T(8,128)(2,1)} %param.11) | copy-start | bytes 2359300
  39.4 5.0 %collective-permute-start.4 = (bf16[128,512]{1,0:T(8,128)(2,1)S(1)}, bf16[128,512]{1,0:T(8,128)(2,1)S(1)}, u32[]{:S(2)}, u32[]{:S(2)}) collective-permute-start(bf16[128,512]{1,0:T(8,128)(2,1)S(1)} %get-tuple-element.15), channel_id=1, source_target_pairs={{0,1},{1,0},{2,3},{3,2},{4,5},{5,4},{6,7},{7,6},{8,9},{9,8},{10,11... | collective-permute-start | bytes 393224 | tf_op jit(solution)/shard_map/ppermute | solution.py:323
  40.0 9.0 %collective-permute-start.5 = (bf16[128,512]{1,0:T(8,128)(2,1)S(1)}, bf16[128,512]{1,0:T(8,128)(2,1)S(1)}, u32[]{:S(2)}, u32[]{:S(2)}) collective-permute-start(bf16[128,512]{1,0:T(8,128)(2,1)S(1)} %get-tuple-element.16), channel_id=1, source_target_pairs={{1,2},{2,1},{3,4},{4,3},{5,6},{6,5},{7,8},{8,7},{9,10},{10,9},{11,... | collective-permute-start | bytes 393224 | tf_op jit(solution)/shard_map/ppermute | solution.py:324

commit v2 on v1

--- a/solution.py
+++ b/solution.py
@@ -67,22 +67,27 @@
 
 
 def atom_kernel(
-    tiles_ref, near_ref, feat_ref, left_ref, own_ref, right_ref, far_ref,
+    tiles_ref, near_hbm, feat_ref, near_a_ref, own_ref, near_b_ref, far_ref,
     wq_ref, wk_ref, wv_ref, wout_ref,
     out_ref, send_a_ref, send_b_ref, mine_ref,
-    table, member, xs, qx, ks, vs, os, acc,
+    table, member, xs, qx, ks, vs, os, acc, near_ref, near_sem,
     *, atoms, tok, ndev,
 ):
     position = lax.axis_index("seq")
+    arrive = pltpu.make_async_copy(near_hbm, near_ref, near_sem)
+    arrive.start()
     tiles = atoms // LANES
     edge = far_ref.shape[0] // 2
     zero = jnp.zeros((LANES - edge, LANES), BF16)
     base = LANES
     table[0 : base - edge, :] = zero
     table[base - edge : base, :] = far_ref[:edge, :]
-    table[base : base + tok, :] = left_ref[:tok, :]
+    odd = lax.rem(position, 2)
+    from_a = pl.multiple_of(base + (1 - odd) * 2 * tok, LANES)
+    from_b = pl.multiple_of(base + odd * 2 * tok, LANES)
+    table[pl.ds(from_a, tok), :] = near_a_ref[:tok, :]
+    table[pl.ds(from_b, tok), :] = near_b_ref[:tok, :]
     table[base + tok : base + 2 * tok, :] = own_ref[...]
-    table[base + 2 * tok : base + 3 * tok, :] = right_ref[:tok, :]
     table[base + 3 * tok : base + 3 * tok + edge, :] = far_ref[edge:, :]
     table[base + 3 * tok + edge :, :] = zero
 
@@ -101,22 +106,26 @@
         got = rows_of(chunk, members(chunk, first, HALO))
         return (feat.astype(F32) + got).astype(BF16)
 
+    is_odd = jnp.full((HALO, LANES), odd, jnp.int32) == 1
+    before = slice(tok + 2 * PAD - HALO, tok + 2 * PAD)
+    after = slice(tok, tok + HALO)
+    arrive.wait()
     xs[0 : PAD - HALO, :] = jnp.zeros((PAD - HALO, LANES), BF16)
     xs[PAD + atoms + HALO :, :] = jnp.zeros((PAD - HALO, LANES), BF16)
-    xs[PAD - HALO : PAD, :] = halo_rows(tiles, -HALO, left_ref[tok + PAD - HALO :, :])
-    xs[PAD + atoms : PAD + atoms + HALO, :] = halo_rows(tiles + 1, atoms, right_ref[tok : tok + HALO, :])
-
-    group = 16
-    pgroup = 16
+    xs[PAD - HALO : PAD, :] = halo_rows(tiles, -HALO, jnp.where(is_odd, near_a_ref[before, :].astype(F32), near_b_ref[before, :].astype(F32)))
+    xs[PAD + atoms : PAD + atoms + HALO, :] = halo_rows(tiles + 1, atoms, jnp.where(is_odd, near_b_ref[after, :].astype(F32), near_a_ref[after, :].astype(F32)))
+
+    group = 32
+    pgroup = 32
 
     def gather(i, carry):
-        for j in range(group):
-            t = i * group + j
-            at = pl.multiple_of(t * LANES, LANES)
-            chunk = tiles_ref[0, t]
-            hit = members(chunk, at, LANES)
+        first = [pl.multiple_of((i * group + j) * LANES, LANES) for j in range(group)]
+        chunk = [tiles_ref[0, i * group + j] for j in range(group)]
+        hits = [members(c, at, LANES) for c, at in zip(chunk, first)]
+        got = [rows_of(c, hit) for c, hit in zip(chunk, hits)]
+        for at, hit, rows in zip(first, hits, got):
             member[pl.ds(at, LANES), :] = hit
-            x = feat_ref[pl.ds(at, LANES), :].astype(F32) + rows_of(chunk, hit)
+            x = feat_ref[pl.ds(at, LANES), :].astype(F32) + rows
             xs[pl.ds(at + PAD, LANES), :] = x.astype(BF16)
         return carry
 
@@ -173,14 +182,13 @@
     group_of = lax.broadcasted_iota(jnp.int32, (head, LANES), 1) // QBLOCK
     blank = jnp.zeros((LANES, LANES), BF16)
 
-    per = 4
+    per = 32
 
     def attend(i, carry):
+        asked, weighed, summed = [], [], []
         for n in range(per):
             at = pl.multiple_of((i * per + n) * LANES, LANES)
             q = qx[:, pl.ds(at, LANES)]
-            value = vs[:, pl.ds(at, 2 * LANES)]
-            parts = []
             for j in (0, 2):
                 key = [ks[pl.ds(at + PAD - HALO + (j + c) * QBLOCK, KEYS), :] for c in range(2)]
                 ask_for = jnp.concatenate(
@@ -190,9 +198,15 @@
                     ],
                     axis=0,
                 )
-                s = jnp.dot(jnp.concatenate(key, axis=1), ask_for, preferred_element_type=F32)
-                top = jnp.max(s, axis=0, keepdims=True)
-                p = jnp.exp2((s - top) * scale).astype(BF16)
+                asked.append(jnp.dot(jnp.concatenate(key, axis=1), ask_for, preferred_element_type=F32))
+        for s in asked:
+            top = jnp.max(s, axis=0, keepdims=True)
+            weighed.append(jnp.exp2((s - top) * scale).astype(BF16))
+        for n in range(per):
+            at = pl.multiple_of((i * per + n) * LANES, LANES)
+            value = vs[:, pl.ds(at, 2 * LANES)]
+            for j in (0, 2):
+                p = weighed[2 * n + j // 2]
                 cols = []
                 for c in range(2):
                     above = PAD - HALO + (j + c) * QBLOCK
@@ -206,8 +220,10 @@
                             axis=0,
                         )
                     )
-                o = jnp.dot(value, jnp.concatenate(cols, axis=1), preferred_element_type=F32)
-                parts += [o[:, :LANES], o[:, LANES:]]
+                summed.append(jnp.dot(value, jnp.concatenate(cols, axis=1), preferred_element_type=F32))
+        for n in range(per):
+            at = pl.multiple_of((i * per + n) * LANES, LANES)
+            parts = [summed[2 * n + j // 2][:, j % 2 * LANES : (j % 2 + 1) * LANES] for j in range(4)]
             for h in range(HEADS):
                 o = parts[0][h * head : (h + 1) * head, :]
                 total = parts[0][LANES : LANES + 1, :]
@@ -234,21 +250,20 @@
     acc[...] = jnp.zeros_like(acc)
 
     def pool(i, carry):
+        parts = []
         for j in range(pgroup):
-            t = i * pgroup + j
-            at = pl.multiple_of(t * LANES, LANES)
-            chunk = tiles_ref[0, t]
-            part = lax.dot_general(
-                out_ref[pl.ds(at, LANES), :], member[pl.ds(at, LANES), :], TN, preferred_element_type=F32
+            at = pl.multiple_of((i * pgroup + j) * LANES, LANES)
+            parts.append(
+                lax.dot_general(
+                    out_ref[pl.ds(at, LANES), :], member[pl.ds(at, LANES), :], TN, preferred_element_type=F32
+                )
             )
-            to = pl.ds(pl.multiple_of(chunk * LANES, LANES), 2 * LANES)
+        for j, part in enumerate(parts):
+            to = pl.ds(pl.multiple_of(tiles_ref[0, i * pgroup + j] * LANES, LANES), 2 * LANES)
             acc[:, to] = acc[:, to] + part
         return carry
 
     lax.fori_loop(0, tiles // pgroup, pool, 0)
-    odd = lax.rem(position, 2)
-    from_a = pl.multiple_of(base + (1 - odd) * 2 * tok, LANES)
-    from_b = pl.multiple_of(base + odd * 2 * tok, LANES)
     send_a_ref[...] = acc[:, pl.ds(from_a, tok)].astype(BF16)
     send_b_ref[...] = acc[:, pl.ds(from_b, tok)].astype(BF16)
     mine_ref[...] = acc[:, base + tok : base + 2 * tok]
@@ -268,8 +283,12 @@
     counts_all = counts_all.reshape(ndev * counts.shape[0], LANES)
 
     proj = jnp.dot(token_cond, w_token, preferred_element_type=F32).astype(BF16)
-    from_left = shifted(jnp.concatenate([proj, atom_feat[atoms - PAD :]]), 1)
-    from_right = shifted(jnp.concatenate([proj, atom_feat[:PAD]]), -1)
+    ends = jnp.concatenate([proj, atom_feat[:PAD], atom_feat[atoms - PAD :]])
+    ends, counts_all = lax.optimization_barrier((ends, counts_all))
+    pairs_a = [(i, i ^ 1) for i in range(ndev)]
+    pairs_b = [(i, ((i + 1) ^ 1) - 1) for i in range(1, ndev - 1)]
+    near_a = lax.ppermute(ends, "seq", pairs_a)
+    near_b = lax.ppermute(ends, "seq", pairs_b)
     whole = pl.BlockSpec(memory_space=pltpu.VMEM)
 
     chunks = 3 * tok // LANES
@@ -282,6 +301,7 @@
         in_specs=[whole],
         out_specs=[whole] + [pl.BlockSpec(memory_space=pltpu.SMEM)],
         scratch_shapes=[pltpu.VMEM((counts_all.shape[0] + 16, LANES), jnp.int32)] * 2,
+        compiler_params=pltpu.CompilerParams(vmem_limit_bytes=2 << 20),
         name="plan",
     )(counts_all)
 
@@ -296,7 +316,7 @@
     window = jax.ShapeDtypeStruct((width, tok), BF16)
     atom_out, send_a, send_b, mine = pl.pallas_call(
         lambda *refs: atom_kernel(*refs, atoms=atoms, tok=tok, ndev=ndev),
-        in_specs=[pl.BlockSpec(memory_space=pltpu.SMEM)] + [vmem] * 10,
+        in_specs=[pl.BlockSpec(memory_space=pltpu.SMEM), pl.BlockSpec(memory_space=pl.ANY)] + [vmem] * 9,
         out_specs=[vmem] * 4,
         out_shape=(
             jax.ShapeDtypeStruct((atoms, width), BF16),
@@ -313,15 +333,17 @@
             pltpu.VMEM((width + ONES, total), BF16),
             pltpu.VMEM((width, atoms), BF16),
             pltpu.VMEM((width, 3 * tok + 2 * LANES), F32),
+            pltpu.VMEM(near.shape, near.dtype),
+            pltpu.SemaphoreType.DMA(()),
         ],
-        compiler_params=pltpu.CompilerParams(vmem_limit_bytes=40 << 20),
+        compiler_params=pltpu.CompilerParams(vmem_limit_bytes=24 << 20),
         name="atoms",
     )(
-        near, near, atom_feat, from_left, proj, from_right, beyond, w_query, w_key, w_value, w_out,
+        near, near, atom_feat, near_a, proj, near_b, beyond, w_query, w_key, w_value, w_out,
     )
 
-    got_a = lax.ppermute(send_a, "seq", [(i, i ^ 1) for i in range(ndev)])
-    got_b = lax.ppermute(send_b, "seq", [(i, ((i + 1) ^ 1) - 1) for i in range(1, ndev - 1)])
+    got_a = lax.ppermute(send_a, "seq", pairs_a)
+    got_b = lax.ppermute(send_b, "seq", pairs_b)
     sums = mine + got_a.astype(F32) + got_b.astype(F32)
     pooled = (sums / atom_counts.astype(F32)[None, :]).astype(BF16)
     token_out = (

time: 50.6 us -> 44.8 us (0.89)
  Pallas kernels: 15 us -> 9.65 us
  waiting for transfers between devices: 11.1 us -> 12.7 us
  starting transfers between devices: 17 us -> 15.5 us
  local copies, waits for them, and re-layouts: 2.83 us -> 2.18 us
    pallas_call x1, Pallas kernels: 13.3 us -> 8.8 us  [shards(): pl.pallas_call(lambda *refs: atom_kernel(*refs, atoms=atoms, tok=tok, nde...]
    ppermute x4, waiting for transfers between devices: 4.91 us -> 8.76 us  [the longest x1 4.02 us: shards(): got_b = lax.ppermute(send_b, 'seq', pairs_b)]
    all_to_all x1, waiting for transfers between devices: 6.24 us -> 3.92 us  [shards(): lax.all_to_all(copies, 'seq', split_axis=0, concat_axis=0, tiled=True)]
    all_to_all x1, starting transfers between devices: 9.65 us -> 7.39 us  [shards(): lax.all_to_all(copies, 'seq', split_axis=0, concat_axis=0, tiled=True)]
    unnamed x20 -> x16, local copies, waits for them, and re-layouts: 1.38 us -> 0.05 us
    pallas_call x1, Pallas kernels: 1.68 us -> 0.85 us  [shards(): pl.pallas_call(lambda *refs: plan_kernel(*refs, atoms=atoms, pad_chunks=1...]
    ppermute x4, starting transfers between devices: 7.34 us -> 8.12 us  [the longest x1 3.98 us: shards(): near_b = lax.ppermute(ends, 'seq', pairs_b)]
    broadcast_in_dim x1, local copies, waits for them, and re-layouts: 0.62 us -> 1.39 us  [shards(): copies = jnp.broadcast_to(counts, (ndev, *counts.shape))]
  transfers between devices with their start and end apart: 5 -> 5, of which waited for: 3 -> 5; matrix products, arithmetic and copies ran while one was open for 1% -> 5% of each run, Pallas kernels for 3% -> 2%
where the time goes in v2:
time: 44.8 us; the launch traced here: 44.3 us
  starting transfers between devices  15.5 us (35%)
  waiting for transfers between devices  12.7 us (28%)
  Pallas kernels  9.65 us (22%)
  matrix products  2.82 us (6%)
  local copies, waits for them, and re-layouts  2.18 us (5%)
  between operations  1.45 us (3%)
    pallas_call x1, Pallas kernels, shards(): pl.pallas_call(lambda *refs: atom_kernel(*refs, atoms=atoms, tok=tok, nde...  8.8 us
    all_to_all x1, starting transfers between devices, shards(): lax.all_to_all(copies, 'seq', split_axis=0, concat_axis=0, tiled=True)  7.39 us
    ppermute x1, waiting for transfers between devices, shards(): got_b = lax.ppermute(send_b, 'seq', pairs_b)  4.02 us
    ppermute x1, starting transfers between devices, shards(): near_b = lax.ppermute(ends, 'seq', pairs_b)  3.98 us
    ppermute x1, starting transfers between devices, shards(): got_b = lax.ppermute(send_b, 'seq', pairs_b)  3.95 us
    all_to_all x1, waiting for transfers between devices, shards(): lax.all_to_all(copies, 'seq', split_axis=0, concat_axis=0, tiled=True)  3.92 us
    ppermute x1, waiting for transfers between devices, shards(): near_b = lax.ppermute(ends, 'seq', pairs_b)  3.68 us
    dot_general x1, matrix products, shards(): proj = jnp.dot(token_cond, w_token, preferred_element_type=F32).astype(BF16)  1.53 us
  transfers between devices with their start and end apart: 5, of which 5 were waited for; matrix products, arithmetic and copies ran while one was open for 5% of the time, Pallas kernels for 2%

profile of v2, /device:TPU:136, one launch (start us, length us, event | category | flops | bytes accessed | tf_op | source)
XLA Modules:
  0.0 44.3 jit_solution(11754299184791440904)
XLA Ops:
  0.6 0.0 copy-start
  0.6 0.0 copy-start.1
  0.7 0.0 copy-start.5
  0.7 0.0 copy-start.4
  0.7 0.0 copy-start.3
  0.7 0.0 copy-start.2
  0.7 1.4 %broadcast_in_dim.4 = s32[16,4,128]{2,1,0:T(4,128)} broadcast(s32[4,128]{1,0:T(4,128)} %bitcast.7), dimensions={1,2} | broadcast | bytes 34816 | tf_op jit(solution)/shard_map/broadcast_in_dim | solution.py:281
  2.1 7.4 %all-to-all-start = ((s32[16,4,128]{2,1,0:T(4,128)}), s32[16,4,128]{2,1,0:T(4,128)S(1)}, u32[]{:S(2)}, u32[]{:S(2)}) async-start(s32[16,4,128]{2,1,0:T(4,128)} %broadcast_in_dim.4), calls=%async_computation | async-start | bytes 65536 | tf_op jit(solution)/shard_map/all_to_all | solution.py:282
  9.5 0.7 %fusion.2 = (bf16[64,128]{1,0:T(8,128)(2,1)S(1)}, bf16[64,128]{1,0:T(8,128)(2,1)S(1)}) fusion(bf16[4096,128]{1,0:T(8,128)(2,1)} %refs_2_.1), kind=kLoop, calls=%fused_computation.7 | loop fusion | bytes 65536 | tf_op jit(solution)/shard_map/slice | solution.py:286
  10.2 1.5 %convolution_convert_fusion.refs_4_ = bf16[512,128]{1,0:T(8,128)(2,1)S(1)} fusion(bf16[512,768]{1,0:T(8,128)(2,1)} %param.11, bf16[768,128]{1,0:T(8,128)(2,1)} %param.14), kind=kOutput, calls=%fused_computation.2 | convolution fusion | flops 100728832 | bytes 1114112 | tf_op jit(solution)/shard_map/dot_general | solution.py:285
  11.8 0.0 copy-start.7
  11.8 0.0 copy-start.6
  11.8 3.9 %all-to-all-done = s32[16,4,128]{2,1,0:T(4,128)S(1)} async-done(((s32[16,4,128]{2,1,0:T(4,128)}), s32[16,4,128]{2,1,0:T(4,128)S(1)}, u32[]{:S(2)}, u32[]{:S(2)}) %all-to-all-start) | async-done | bytes 32800 | tf_op jit(solution)/shard_map/all_to_all | solution.py:282
  15.7 4.0 %collective-permute-start.3 = (bf16[640,128]{1,0:T(8,128)(2,1)S(1)}, bf16[640,128]{1,0:T(8,128)(2,1)S(1)}, u32[]{:S(2)}, u32[]{:S(2)}) collective-permute-start(bf16[640,128]{1,0:T(8,128)(2,1)S(1)} %pad_maximum_fusion.1), channel_id=1, source_target_pairs={{1,2},{2,1},{3,4},{4,3},{5,6},{6,5},{7,8},{8,7},{9,10},{10,9},{11,... | collective-permute-start | bytes 491528 | tf_op jit(solution)/shard_map/ppermute | solution.py:291
  19.7 0.1 collective-permute-start.2
  19.8 0.9 %plan.1 = (s32[40,128]{1,0:T(8,128)S(1)}, s32[1,1]{1,0:T(1,128)}) custom-call(s32[64,128]{1,0:T(8,128)S(1)} %bitcast.6), custom_call_target="tpu_custom_call" | custom-call | tf_op jit(solution)/shard_map/plan/pallas_call | solution.py:295
  21.4 3.7 %collective-permute-done.3.refs_5_ = bf16[640,128]{1,0:T(8,128)(2,1)S(1)} collective-permute-done((bf16[640,128]{1,0:T(8,128)(2,1)S(1)}, bf16[640,128]{1,0:T(8,128)(2,1)S(1)}, u32[]{:S(2)}, u32[]{:S(2)}) %collective-permute-start.3) | collective-permute-done | bytes 163872 | tf_op jit(solution)/shard_map/ppermute | solution.py:291
  25.0 0.1 collective-permute-done.2.refs_3_
  25.1 0.0 copy-done.1
  25.1 0.0 copy-done.5
  25.1 0.0 copy-done.4
  25.1 0.0 copy-done.3
  25.1 0.0 copy-done.2
  25.2 8.8 %atoms.1 = (bf16[4096,128]{1,0:T(8,128)(2,1)}, bf16[128,512]{1,0:T(8,128)(2,1)S(1)}, bf16[128,512]{1,0:T(8,128)(2,1)S(1)}, f32[128,512]{1,0:T(8,128)S(1)}) custom-call(s32[40,128]{1,0:T(8,128)S(1)} %get-tuple-element.15.refs_0_.refs_1_, s32[40,128]{1,0:T(8,128)S(1)} %get-tuple-element.15.refs_0_.refs_1_, bf16[4096,128]{1,0:T(8,128)(2,1)S(1)} %copy-done.1, ...), custom_call_target="tpu_custom_call" | custom-call | tf_op jit(solution)/shard_map/atoms/pallas_call | solution.py:317
  34.0 0.1 collective-permute-start.4
  34.1 3.9 %collective-permute-start.5 = (bf16[128,512]{1,0:T(8,128)(2,1)S(1)}, bf16[128,512]{1,0:T(8,128)(2,1)S(1)}, u32[]{:S(2)}, u32[]{:S(2)}) collective-permute-start(bf16[128,512]{1,0:T(8,128)(2,1)S(1)} %get-tuple-element.20), channel_id=1, source_target_pairs={{1,2},{2,1},{3,4},{4,3},{5,6},{6,5},{7,8},{8,7},{9,10},{10,9},{11,... | collective-permute-start | bytes 393224 | tf_op jit(solution)/shard_map/ppermute | solution.py:346
  38.0 0.0 copy-done.7
  38.0 1.0 %collective-permute-done.4 = bf16[128,512]{1,0:T(8,128)(2,1)S(1)} collective-permute-done((bf16[128,512]{1,0:T(8,128)(2,1)S(1)}, bf16[128,512]{1,0:T(8,128)(2,1)S(1)}, u32[]{:S(2)}, u32[]{:S(2)}) %collective-permute-start.4) | collective-permute-done | bytes 131104 | tf_op jit(solution)/shard_map/ppermute | solution.py:345
  39.0 4.0 %collective-permute-done.5 = bf16[128,512]{1,0:T(8,128)(2,1)S(1)} collective-permute-done((bf16[128,512]{1,0:T(8,128)(2,1)S(1)}, bf16[128,512]{1,0:T(8,128)(2,1)S(1)}, u32[]{:S(2)}, u32[]{:S(2)}) %collective-permute-start.5) | collective-permute-done | bytes 131104 | tf_op jit(solution)/shard_map/ppermute | solution.py:346
  43.0 0.0 copy-done
  43.0 0.0 copy-done.6
  43.0 1.3 %add_convert_fusion = bf16[512,768]{1,0:T(8,128)(2,1)} fusion(bf16[512,768]{1,0:T(8,128)(2,1)S(1)} %copy-done.6, bf16[128,768]{1,0:T(8,128)(2,1)S(1)} %copy-done, bf16[128,512]{1,0:T(8,128)(2,1)S(1)} %collective-permute-done.5, f32[128,512]{1,0:T(8,128)S(1)} %get-tuple-element.18, bf16[128,512]{1,0:T(8,128)(2,1)S(1)} %collective-permute-done.4, ...), kind=kOutput, calls=%fused_computation.1 | convolution fusion | flops 102236160 | bytes 2295808 | tf_op jit(solution)/shard_map/dot_general | solution.py:350
  (4 shorter events, 0.0 us)
Async XLA Ops:
  0.6 42.4 %copy-start = (bf16[128,768]{1,0:T(8,128)(2,1)S(1)}, bf16[128,768]{1,0:T(8,128)(2,1)}, u32[]{:S(2)}) copy-start(bf16[128,768]{1,0:T(8,128)(2,1)} %param.19) | copy-start | bytes 589828
  0.6 24.5 %copy-start.1 = (bf16[4096,128]{1,0:T(8,128)(2,1)S(1)}, bf16[4096,128]{1,0:T(8,128)(2,1)}, u32[]{:S(2)}) copy-start(bf16[4096,128]{1,0:T(8,128)(2,1)} %refs_2_.1) | copy-start | bytes 3145732
  0.7 24.5 %copy-start.5 = (bf16[128,128]{1,0:T(8,128)(2,1)S(1)}, bf16[128,128]{1,0:T(8,128)(2,1)}, u32[]{:S(2)}) copy-start(bf16[128,128]{1,0:T(8,128)(2,1)} %refs_10_.1) | copy-start | bytes 98308
  0.7 24.5 %copy-start.4 = (bf16[128,128]{1,0:T(8,128)(2,1)S(1)}, bf16[128,128]{1,0:T(8,128)(2,1)}, u32[]{:S(2)}) copy-start(bf16[128,128]{1,0:T(8,128)(2,1)} %refs_9_.1) | copy-start | bytes 98308
  0.7 24.5 %copy-start.3 = (bf16[128,128]{1,0:T(8,128)(2,1)S(1)}, bf16[128,128]{1,0:T(8,128)(2,1)}, u32[]{:S(2)}) copy-start(bf16[128,128]{1,0:T(8,128)(2,1)} %refs_8_.1) | copy-start | bytes 98308
  0.7 24.5 %copy-start.2 = (bf16[128,128]{1,0:T(8,128)(2,1)S(1)}, bf16[128,128]{1,0:T(8,128)(2,1)}, u32[]{:S(2)}) copy-start(bf16[128,128]{1,0:T(8,128)(2,1)} %refs_7_.1) | copy-start | bytes 98308
  2.1 13.6 %all-to-all-start = ((s32[16,4,128]{2,1,0:T(4,128)}), s32[16,4,128]{2,1,0:T(4,128)S(1)}, u32[]{:S(2)}, u32[]{:S(2)}) async-start(s32[16,4,128]{2,1,0:T(4,128)} %broadcast_in_dim.4), calls=%async_computation | async-start | bytes 65536 | tf_op jit(solution)/shard_map/all_to_all | solution.py:282
  11.8 26.3 %copy-start.7 = (s32[512]{0:T(512)S(1)}, s32[512]{0:T(512)}, u32[]{:S(2)}) copy-start(s32[512]{0:T(512)} %param.13) | copy-start | bytes 6148
  11.8 31.3 %copy-start.6 = (bf16[512,768]{1,0:T(8,128)(2,1)S(1)}, bf16[512,768]{1,0:T(8,128)(2,1)}, u32[]{:S(2)}) copy-start(bf16[512,768]{1,0:T(8,128)(2,1)} %param.11) | copy-start | bytes 2359300
  15.7 9.3 %collective-permute-start.3 = (bf16[640,128]{1,0:T(8,128)(2,1)S(1)}, bf16[640,128]{1,0:T(8,128)(2,1)S(1)}, u32[]{:S(2)}, u32[]{:S(2)}) collective-permute-start(bf16[640,128]{1,0:T(8,128)(2,1)S(1)} %pad_maximum_fusion.1), channel_id=1, source_target_pairs={{1,2},{2,1},{3,4},{4,3},{5,6},{6,5},{7,8},{8,7},{9,10},{10,9},{11,... | collective-permute-start | bytes 491528 | tf_op jit(solution)/shard_map/ppermute | solution.py:291
  19.7 5.4 %collective-permute-start.2 = (bf16[640,128]{1,0:T(8,128)(2,1)S(1)}, bf16[640,128]{1,0:T(8,128)(2,1)S(1)}, u32[]{:S(2)}, u32[]{:S(2)}) collective-permute-start(bf16[640,128]{1,0:T(8,128)(2,1)S(1)} %pad_maximum_fusion.1), channel_id=1, source_target_pairs={{0,1},{1,0},{2,3},{3,2},{4,5},{5,4},{6,7},{7,6},{8,9},{9,8},{10,11... | collective-permute-start | bytes 491528 | tf_op jit(solution)/shard_map/ppermute | solution.py:290
  34.0 5.1 %collective-permute-start.4 = (bf16[128,512]{1,0:T(8,128)(2,1)S(1)}, bf16[128,512]{1,0:T(8,128)(2,1)S(1)}, u32[]{:S(2)}, u32[]{:S(2)}) collective-permute-start(bf16[128,512]{1,0:T(8,128)(2,1)S(1)} %get-tuple-element.19), channel_id=1, source_target_pairs={{0,1},{1,0},{2,3},{3,2},{4,5},{5,4},{6,7},{7,6},{8,9},{9,8},{10,11... | collective-permute-start | bytes 393224 | tf_op jit(solution)/shard_map/ppermute | solution.py:345
  34.1 9.0 %collective-permute-start.5 = (bf16[128,512]{1,0:T(8,128)(2,1)S(1)}, bf16[128,512]{1,0:T(8,128)(2,1)S(1)}, u32[]{:S(2)}, u32[]{:S(2)}) collective-permute-start(bf16[128,512]{1,0:T(8,128)(2,1)S(1)} %get-tuple-element.20), channel_id=1, source_target_pairs={{1,2},{2,1},{3,4},{4,3},{5,6},{6,5},{7,8},{8,7},{9,10},{10,9},{11,... | collective-permute-start | bytes 393224 | tf_op jit(solution)/shard_map/ppermute | solution.py:346

commit v3 on v2

--- a/solution.py
+++ b/solution.py
@@ -286,9 +286,16 @@
     ends = jnp.concatenate([proj, atom_feat[:PAD], atom_feat[atoms - PAD :]])
     ends, counts_all = lax.optimization_barrier((ends, counts_all))
     pairs_a = [(i, i ^ 1) for i in range(ndev)]
-    pairs_b = [(i, ((i + 1) ^ 1) - 1) for i in range(1, ndev - 1)]
+    pairs_b = [
+        (
+            part * ndev + i,
+            part * ndev + ((i + 1) ^ 1) - 1 if 0 < i < ndev - 1 else (part ^ 1) * ndev + i,
+        )
+        for part in range(lax.axis_size("batch"))
+        for i in range(ndev)
+    ]
     near_a = lax.ppermute(ends, "seq", pairs_a)
-    near_b = lax.ppermute(ends, "seq", pairs_b)
+    near_b = lax.ppermute(ends, ("batch", "seq"), pairs_b)
     whole = pl.BlockSpec(memory_space=pltpu.VMEM)
 
     chunks = 3 * tok // LANES
@@ -343,7 +350,7 @@
     )
 
     got_a = lax.ppermute(send_a, "seq", pairs_a)
-    got_b = lax.ppermute(send_b, "seq", pairs_b)
+    got_b = lax.ppermute(send_b, ("batch", "seq"), pairs_b)
     sums = mine + got_a.astype(F32) + got_b.astype(F32)
     pooled = (sums / atom_counts.astype(F32)[None, :]).astype(BF16)
     token_out = (

time: 44.8 us -> 40.9 us (0.913)
  starting transfers between devices: 15.5 us -> 11.8 us
    ppermute x2, starting transfers between devices: 7.93 us -> 4.26 us  [the longest x1 2.18 us: shards(): got_b = lax.ppermute(send_b, ('batch', 'seq'), pairs_b)]
    ppermute x1, waiting for transfers between devices: 0.98 us -> 2.77 us  [shards(): got_a = lax.ppermute(send_a, 'seq', pairs_a)]
    ppermute x2, waiting for transfers between devices: 7.69 us -> 6.01 us  [the longest x1 3.8 us: shards(): near_b = lax.ppermute(ends, ('batch', 'seq'), pairs_b)]
  transfers between devices with their start and end apart: 5 -> 5, of which waited for: 5 -> 4; matrix products, arithmetic and copies ran while one was open for 5% -> 6% of each run, Pallas kernels for 2% -> 2%
where the time goes in v3:
time: 40.9 us; the launch traced here: 40.6 us
  waiting for transfers between devices  12.7 us (31%)
  starting transfers between devices  11.8 us (29%)
  Pallas kernels  9.64 us (24%)
  matrix products  2.82 us (7%)
  local copies, waits for them, and re-layouts  2.18 us (5%)
  between operations  1.42 us (3%)
    pallas_call x1, Pallas kernels, shards(): pl.pallas_call(lambda *refs: atom_kernel(*refs, atoms=atoms, tok=tok, nde...  8.79 us
    all_to_all x1, starting transfers between devices, shards(): lax.all_to_all(copies, 'seq', split_axis=0, concat_axis=0, tiled=True)  7.39 us
    all_to_all x1, waiting for transfers between devices, shards(): lax.all_to_all(copies, 'seq', split_axis=0, concat_axis=0, tiled=True)  3.92 us
    ppermute x1, waiting for transfers between devices, shards(): near_b = lax.ppermute(ends, ('batch', 'seq'), pairs_b)  3.8 us
    ppermute x1, waiting for transfers between devices, shards(): got_a = lax.ppermute(send_a, 'seq', pairs_a)  2.77 us
    ppermute x1, waiting for transfers between devices, shards(): got_b = lax.ppermute(send_b, ('batch', 'seq'), pairs_b)  2.21 us
    ppermute x1, starting transfers between devices, shards(): got_b = lax.ppermute(send_b, ('batch', 'seq'), pairs_b)  2.18 us
    ppermute x1, starting transfers between devices, shards(): near_b = lax.ppermute(ends, ('batch', 'seq'), pairs_b)  2.09 us
  transfers between devices with their start and end apart: 5, of which 4 were waited for; matrix products, arithmetic and copies ran while one was open for 6% of the time, Pallas kernels for 2%

profile of v3, /device:TPU:136, one launch (start us, length us, event | category | flops | bytes accessed | tf_op | source)
XLA Modules:
  0.0 40.6 jit_solution(9677920390372688834)
XLA Ops:
  0.6 0.0 copy-start
  0.6 0.0 copy-start.1
  0.7 0.0 copy-start.5
  0.7 0.0 copy-start.4
  0.7 0.0 copy-start.3
  0.7 0.0 copy-start.2
  0.7 1.4 %broadcast_in_dim.4 = s32[16,4,128]{2,1,0:T(4,128)} broadcast(s32[4,128]{1,0:T(4,128)} %bitcast.7), dimensions={1,2} | broadcast | bytes 34816 | tf_op jit(solution)/shard_map/broadcast_in_dim | solution.py:281
  2.1 7.4 %all-to-all-start = ((s32[16,4,128]{2,1,0:T(4,128)}), s32[16,4,128]{2,1,0:T(4,128)S(1)}, u32[]{:S(2)}, u32[]{:S(2)}) async-start(s32[16,4,128]{2,1,0:T(4,128)} %broadcast_in_dim.4), calls=%async_computation | async-start | bytes 65536 | tf_op jit(solution)/shard_map/all_to_all | solution.py:282
  9.5 0.7 %fusion.2 = (bf16[64,128]{1,0:T(8,128)(2,1)S(1)}, bf16[64,128]{1,0:T(8,128)(2,1)S(1)}) fusion(bf16[4096,128]{1,0:T(8,128)(2,1)} %refs_2_.1), kind=kLoop, calls=%fused_computation.7 | loop fusion | bytes 65536 | tf_op jit(solution)/shard_map/slice | solution.py:286
  10.2 1.5 %convolution_convert_fusion.refs_4_ = bf16[512,128]{1,0:T(8,128)(2,1)S(1)} fusion(bf16[512,768]{1,0:T(8,128)(2,1)} %param.11, bf16[768,128]{1,0:T(8,128)(2,1)} %param.14), kind=kOutput, calls=%fused_computation.2 | convolution fusion | flops 100728832 | bytes 1114112 | tf_op jit(solution)/shard_map/dot_general | solution.py:285
  11.8 0.0 copy-start.7
  11.8 0.0 copy-start.6
  11.8 3.9 %all-to-all-done = s32[16,4,128]{2,1,0:T(4,128)S(1)} async-done(((s32[16,4,128]{2,1,0:T(4,128)}), s32[16,4,128]{2,1,0:T(4,128)S(1)}, u32[]{:S(2)}, u32[]{:S(2)}) %all-to-all-start) | async-done | bytes 32800 | tf_op jit(solution)/shard_map/all_to_all | solution.py:282
  15.7 2.1 %collective-permute-start.3 = (bf16[640,128]{1,0:T(8,128)(2,1)S(1)}, bf16[640,128]{1,0:T(8,128)(2,1)S(1)}, u32[]{:S(2)}, u32[]{:S(2)}) collective-permute-start(bf16[640,128]{1,0:T(8,128)(2,1)S(1)} %pad_maximum_fusion.1), channel_id=1, source_target_pairs={{0,16},{1,2},{2,1},{3,4},{4,3},{5,6},{6,5},{7,8},{8,7},{9,10},{10,... | collective-permute-start | bytes 491528 | tf_op jit(solution)/shard_map/ppermute | solution.py:298
  17.8 0.0 collective-permute-start.2
  17.8 0.9 %plan.1 = (s32[40,128]{1,0:T(8,128)S(1)}, s32[1,1]{1,0:T(1,128)}) custom-call(s32[64,128]{1,0:T(8,128)S(1)} %bitcast.6), custom_call_target="tpu_custom_call" | custom-call | tf_op jit(solution)/shard_map/plan/pallas_call | solution.py:302
  19.4 3.8 %collective-permute-done.3.refs_5_ = bf16[640,128]{1,0:T(8,128)(2,1)S(1)} collective-permute-done((bf16[640,128]{1,0:T(8,128)(2,1)S(1)}, bf16[640,128]{1,0:T(8,128)(2,1)S(1)}, u32[]{:S(2)}, u32[]{:S(2)}) %collective-permute-start.3) | collective-permute-done | bytes 163872 | tf_op jit(solution)/shard_map/ppermute | solution.py:298
  23.2 0.0 collective-permute-done.2.refs_3_
  23.2 0.0 copy-done.1
  23.2 0.0 copy-done.5
  23.2 0.0 copy-done.4
  23.2 0.0 copy-done.3
  23.2 0.0 copy-done.2
  23.2 8.8 %atoms.1 = (bf16[4096,128]{1,0:T(8,128)(2,1)}, bf16[128,512]{1,0:T(8,128)(2,1)S(1)}, bf16[128,512]{1,0:T(8,128)(2,1)S(1)}, f32[128,512]{1,0:T(8,128)S(1)}) custom-call(s32[40,128]{1,0:T(8,128)S(1)} %get-tuple-element.15.refs_0_.refs_1_, s32[40,128]{1,0:T(8,128)S(1)} %get-tuple-element.15.refs_0_.refs_1_, bf16[4096,128]{1,0:T(8,128)(2,1)S(1)} %copy-done.1, ...), custom_call_target="tpu_custom_call" | custom-call | tf_op jit(solution)/shard_map/atoms/pallas_call | solution.py:324
  32.0 0.1 collective-permute-start.4
  32.1 2.2 %collective-permute-start.5 = (bf16[128,512]{1,0:T(8,128)(2,1)S(1)}, bf16[128,512]{1,0:T(8,128)(2,1)S(1)}, u32[]{:S(2)}, u32[]{:S(2)}) collective-permute-start(bf16[128,512]{1,0:T(8,128)(2,1)S(1)} %get-tuple-element.20), channel_id=1, source_target_pairs={{0,16},{1,2},{2,1},{3,4},{4,3},{5,6},{6,5},{7,8},{8,7},{9,10},{10,... | collective-permute-start | bytes 393224 | tf_op jit(solution)/shard_map/ppermute | solution.py:353
  34.3 0.0 copy-done.7
  34.3 2.8 %collective-permute-done.4 = bf16[128,512]{1,0:T(8,128)(2,1)S(1)} collective-permute-done((bf16[128,512]{1,0:T(8,128)(2,1)S(1)}, bf16[128,512]{1,0:T(8,128)(2,1)S(1)}, u32[]{:S(2)}, u32[]{:S(2)}) %collective-permute-start.4) | collective-permute-done | bytes 131104 | tf_op jit(solution)/shard_map/ppermute | solution.py:352
  37.1 2.2 %collective-permute-done.5 = bf16[128,512]{1,0:T(8,128)(2,1)S(1)} collective-permute-done((bf16[128,512]{1,0:T(8,128)(2,1)S(1)}, bf16[128,512]{1,0:T(8,128)(2,1)S(1)}, u32[]{:S(2)}, u32[]{:S(2)}) %collective-permute-start.5) | collective-permute-done | bytes 131104 | tf_op jit(solution)/shard_map/ppermute | solution.py:353
  39.3 0.0 copy-done
  39.3 0.0 copy-done.6
  39.3 1.3 %add_convert_fusion = bf16[512,768]{1,0:T(8,128)(2,1)} fusion(bf16[512,768]{1,0:T(8,128)(2,1)S(1)} %copy-done.6, bf16[128,768]{1,0:T(8,128)(2,1)S(1)} %copy-done, bf16[128,512]{1,0:T(8,128)(2,1)S(1)} %collective-permute-done.5, f32[128,512]{1,0:T(8,128)S(1)} %get-tuple-element.18, bf16[128,512]{1,0:T(8,128)(2,1)S(1)} %collective-permute-done.4, ...), kind=kOutput, calls=%fused_computation.1 | convolution fusion | flops 102236160 | bytes 2295808 | tf_op jit(solution)/shard_map/dot_general | solution.py:357
  (4 shorter events, 0.0 us)
Async XLA Ops:
  0.6 38.6 %copy-start = (bf16[128,768]{1,0:T(8,128)(2,1)S(1)}, bf16[128,768]{1,0:T(8,128)(2,1)}, u32[]{:S(2)}) copy-start(bf16[128,768]{1,0:T(8,128)(2,1)} %param.19) | copy-start | bytes 589828
  0.6 22.5 %copy-start.1 = (bf16[4096,128]{1,0:T(8,128)(2,1)S(1)}, bf16[4096,128]{1,0:T(8,128)(2,1)}, u32[]{:S(2)}) copy-start(bf16[4096,128]{1,0:T(8,128)(2,1)} %refs_2_.1) | copy-start | bytes 3145732
  0.7 22.5 %copy-start.5 = (bf16[128,128]{1,0:T(8,128)(2,1)S(1)}, bf16[128,128]{1,0:T(8,128)(2,1)}, u32[]{:S(2)}) copy-start(bf16[128,128]{1,0:T(8,128)(2,1)} %refs_10_.1) | copy-start | bytes 98308
  0.7 22.5 %copy-start.4 = (bf16[128,128]{1,0:T(8,128)(2,1)S(1)}, bf16[128,128]{1,0:T(8,128)(2,1)}, u32[]{:S(2)}) copy-start(bf16[128,128]{1,0:T(8,128)(2,1)} %refs_9_.1) | copy-start | bytes 98308
  0.7 22.5 %copy-start.3 = (bf16[128,128]{1,0:T(8,128)(2,1)S(1)}, bf16[128,128]{1,0:T(8,128)(2,1)}, u32[]{:S(2)}) copy-start(bf16[128,128]{1,0:T(8,128)(2,1)} %refs_8_.1) | copy-start | bytes 98308
  0.7 22.5 %copy-start.2 = (bf16[128,128]{1,0:T(8,128)(2,1)S(1)}, bf16[128,128]{1,0:T(8,128)(2,1)}, u32[]{:S(2)}) copy-start(bf16[128,128]{1,0:T(8,128)(2,1)} %refs_7_.1) | copy-start | bytes 98308
  2.1 13.6 %all-to-all-start = ((s32[16,4,128]{2,1,0:T(4,128)}), s32[16,4,128]{2,1,0:T(4,128)S(1)}, u32[]{:S(2)}, u32[]{:S(2)}) async-start(s32[16,4,128]{2,1,0:T(4,128)} %broadcast_in_dim.4), calls=%async_computation | async-start | bytes 65536 | tf_op jit(solution)/shard_map/all_to_all | solution.py:282
  11.8 22.5 %copy-start.7 = (s32[512]{0:T(512)S(1)}, s32[512]{0:T(512)}, u32[]{:S(2)}) copy-start(s32[512]{0:T(512)} %param.13) | copy-start | bytes 6148
  11.8 27.5 %copy-start.6 = (bf16[512,768]{1,0:T(8,128)(2,1)S(1)}, bf16[512,768]{1,0:T(8,128)(2,1)}, u32[]{:S(2)}) copy-start(bf16[512,768]{1,0:T(8,128)(2,1)} %param.11) | copy-start | bytes 2359300
  15.7 7.4 %collective-permute-start.3 = (bf16[640,128]{1,0:T(8,128)(2,1)S(1)}, bf16[640,128]{1,0:T(8,128)(2,1)S(1)}, u32[]{:S(2)}, u32[]{:S(2)}) collective-permute-start(bf16[640,128]{1,0:T(8,128)(2,1)S(1)} %pad_maximum_fusion.1), channel_id=1, source_target_pairs={{0,16},{1,2},{2,1},{3,4},{4,3},{5,6},{6,5},{7,8},{8,7},{9,10},{10,... | collective-permute-start | bytes 491528 | tf_op jit(solution)/shard_map/ppermute | solution.py:298
  17.8 5.3 %collective-permute-start.2 = (bf16[640,128]{1,0:T(8,128)(2,1)S(1)}, bf16[640,128]{1,0:T(8,128)(2,1)S(1)}, u32[]{:S(2)}, u32[]{:S(2)}) collective-permute-start(bf16[640,128]{1,0:T(8,128)(2,1)S(1)} %pad_maximum_fusion.1), channel_id=1, source_target_pairs={{0,1},{1,0},{2,3},{3,2},{4,5},{5,4},{6,7},{7,6},{8,9},{9,8},{10,11... | collective-permute-start | bytes 491528 | tf_op jit(solution)/shard_map/ppermute | solution.py:297
  32.0 5.1 %collective-permute-start.4 = (bf16[128,512]{1,0:T(8,128)(2,1)S(1)}, bf16[128,512]{1,0:T(8,128)(2,1)S(1)}, u32[]{:S(2)}, u32[]{:S(2)}) collective-permute-start(bf16[128,512]{1,0:T(8,128)(2,1)S(1)} %get-tuple-element.19), channel_id=1, source_target_pairs={{0,1},{1,0},{2,3},{3,2},{4,5},{5,4},{6,7},{7,6},{8,9},{9,8},{10,11... | collective-permute-start | bytes 393224 | tf_op jit(solution)/shard_map/ppermute | solution.py:352
  32.1 7.2 %collective-permute-start.5 = (bf16[128,512]{1,0:T(8,128)(2,1)S(1)}, bf16[128,512]{1,0:T(8,128)(2,1)S(1)}, u32[]{:S(2)}, u32[]{:S(2)}) collective-permute-start(bf16[128,512]{1,0:T(8,128)(2,1)S(1)} %get-tuple-element.20), channel_id=1, source_target_pairs={{0,16},{1,2},{2,1},{3,4},{4,3},{5,6},{6,5},{7,8},{8,7},{9,10},{10,... | collective-permute-start | bytes 393224 | tf_op jit(solution)/shard_map/ppermute | solution.py:353

commit v4 on v3

--- a/solution.py
+++ b/solution.py
@@ -284,7 +284,6 @@
 
     proj = jnp.dot(token_cond, w_token, preferred_element_type=F32).astype(BF16)
     ends = jnp.concatenate([proj, atom_feat[:PAD], atom_feat[atoms - PAD :]])
-    ends, counts_all = lax.optimization_barrier((ends, counts_all))
     pairs_a = [(i, i ^ 1) for i in range(ndev)]
     pairs_b = [
         (

time: 40.9 us -> 39.5 us (0.966)
  waiting for transfers between devices: 12.7 us -> 11.2 us
  starting transfers between devices: 11.8 us -> 12.7 us
  local copies, waits for them, and re-layouts: 2.18 us -> 1.5 us
    ppermute x1, waiting for transfers between devices: 3.8 us -> 0.01 us  [shards(): near_b = lax.ppermute(ends, ('batch', 'seq'), pairs_b)]
    all_to_all x1, waiting for transfers between devices: 3.92 us -> 6.24 us  [shards(): lax.all_to_all(copies, 'seq', split_axis=0, concat_axis=0, tiled=True)]
    broadcast_in_dim x1, local copies, waits for them, and re-layouts: 1.39 us -> 0.62 us  [shards(): copies = jnp.broadcast_to(counts, (ndev, *counts.shape))]
    ppermute x1, starting transfers between devices: 2.09 us -> 2.73 us  [shards(): near_b = lax.ppermute(ends, ('batch', 'seq'), pairs_b)]
    all_to_all x1, starting transfers between devices: 7.39 us -> 6.81 us  [shards(): lax.all_to_all(copies, 'seq', split_axis=0, concat_axis=0, tiled=True)]
    ppermute x1, starting transfers between devices: 0.09 us -> 0.67 us  [shards(): got_a = lax.ppermute(send_a, 'seq', pairs_a)]
    ppermute x1, waiting for transfers between devices: 2.77 us -> 2.24 us  [shards(): got_a = lax.ppermute(send_a, 'seq', pairs_a)]
    ppermute x1, waiting for transfers between devices: 2.21 us -> 2.69 us  [shards(): got_b = lax.ppermute(send_b, ('batch', 'seq'), pairs_b)]
  transfers between devices with their start and end apart: 5 -> 5, of which waited for: 4 -> 3; matrix products, arithmetic and copies ran while one was open for 6% -> 2% of each run, Pallas kernels for 2% -> 2%
where the time goes in v4:
time: 39.5 us; the launch traced here: 39.3 us
  starting transfers between devices  12.7 us (32%)
  waiting for transfers between devices  11.2 us (28%)
  Pallas kernels  9.64 us (24%)
  matrix products  2.82 us (7%)
  local copies, waits for them, and re-layouts  1.5 us (4%)
  between operations  1.44 us (4%)
    pallas_call x1, Pallas kernels, shards(): pl.pallas_call(lambda *refs: atom_kernel(*refs, atoms=atoms, tok=tok, nde...  8.79 us
    all_to_all x1, starting transfers between devices, shards(): lax.all_to_all(copies, 'seq', split_axis=0, concat_axis=0, tiled=True)  6.81 us
    all_to_all x1, waiting for transfers between devices, shards(): lax.all_to_all(copies, 'seq', split_axis=0, concat_axis=0, tiled=True)  6.24 us
    ppermute x1, starting transfers between devices, shards(): near_b = lax.ppermute(ends, ('batch', 'seq'), pairs_b)  2.73 us
    ppermute x1, waiting for transfers between devices, shards(): got_b = lax.ppermute(send_b, ('batch', 'seq'), pairs_b)  2.69 us
    ppermute x1, waiting for transfers between devices, shards(): got_a = lax.ppermute(send_a, 'seq', pairs_a)  2.24 us
    ppermute x1, starting transfers between devices, shards(): got_b = lax.ppermute(send_b, ('batch', 'seq'), pairs_b)  2.15 us
    dot_general x1, matrix products, shards(): proj = jnp.dot(token_cond, w_token, preferred_element_type=F32).astype(BF16)  1.53 us
  transfers between devices with their start and end apart: 5, of which 3 were waited for; matrix products, arithmetic and copies ran while one was open for 2% of the time, Pallas kernels for 2%

profile of v4, /device:TPU:136, one launch (start us, length us, event | category | flops | bytes accessed | tf_op | source)
XLA Modules:
  0.0 39.3 jit_solution(4807849546161535790)
XLA Ops:
  0.6 0.0 copy-start
  0.6 0.0 copy-start.1
  0.7 0.0 copy-start.7
  0.7 0.0 copy-start.5
  0.7 0.0 copy-start.4
  0.7 0.0 copy-start.3
  0.7 0.0 copy-start.2
  0.7 0.8 %fusion.2 = (bf16[64,128]{1,0:T(8,128)(2,1)S(1)}, bf16[64,128]{1,0:T(8,128)(2,1)S(1)}) fusion(bf16[4096,128]{1,0:T(8,128)(2,1)} %refs_2_.1), kind=kLoop, calls=%fused_computation.7 | loop fusion | bytes 65536 | tf_op jit(solution)/shard_map/slice | solution.py:286
  1.5 1.5 %convolution_convert_fusion.refs_4_ = bf16[512,128]{1,0:T(8,128)(2,1)S(1)} fusion(bf16[512,768]{1,0:T(8,128)(2,1)} %param.11, bf16[768,128]{1,0:T(8,128)(2,1)} %param.14), kind=kOutput, calls=%fused_computation.2 | convolution fusion | flops 100728832 | bytes 1114112 | tf_op jit(solution)/shard_map/dot_general | solution.py:285
  3.1 0.0 copy-start.6
  3.1 2.7 %collective-permute-start.3 = (bf16[640,128]{1,0:T(8,128)(2,1)S(1)}, bf16[640,128]{1,0:T(8,128)(2,1)S(1)}, u32[]{:S(2)}, u32[]{:S(2)}) collective-permute-start(bf16[640,128]{1,0:T(8,128)(2,1)S(1)} %pad_maximum_fusion.1), channel_id=1, source_target_pairs={{0,16},{1,2},{2,1},{3,4},{4,3},{5,6},{6,5},{7,8},{8,7},{9,10},{10,... | collective-permute-start | bytes 491528 | tf_op jit(solution)/shard_map/ppermute | solution.py:297
  5.8 0.3 collective-permute-start.2
  6.2 0.0 copy-done.7
  6.2 0.6 %broadcast_in_dim.4 = s32[16,4,128]{2,1,0:T(4,128)} broadcast(s32[4,128]{1,0:T(4,128)S(1)} %bitcast.7), dimensions={1,2} | broadcast | bytes 34816 | tf_op jit(solution)/shard_map/broadcast_in_dim | solution.py:281
  6.8 6.8 %all-to-all-start = ((s32[16,4,128]{2,1,0:T(4,128)}), s32[16,4,128]{2,1,0:T(4,128)S(1)}, u32[]{:S(2)}, u32[]{:S(2)}) async-start(s32[16,4,128]{2,1,0:T(4,128)} %broadcast_in_dim.4), calls=%async_computation | async-start | bytes 65536 | tf_op jit(solution)/shard_map/all_to_all | solution.py:282
  13.6 6.2 %all-to-all-done = s32[16,4,128]{2,1,0:T(4,128)S(1)} async-done(((s32[16,4,128]{2,1,0:T(4,128)}), s32[16,4,128]{2,1,0:T(4,128)S(1)}, u32[]{:S(2)}, u32[]{:S(2)}) %all-to-all-start) | async-done | bytes 32800 | tf_op jit(solution)/shard_map/all_to_all | solution.py:282
  19.8 0.9 %plan.1 = (s32[40,128]{1,0:T(8,128)S(1)}, s32[1,1]{1,0:T(1,128)}) custom-call(s32[64,128]{1,0:T(8,128)S(1)} %bitcast.6), custom_call_target="tpu_custom_call" | custom-call | tf_op jit(solution)/shard_map/plan/pallas_call | solution.py:301
  21.4 0.0 collective-permute-done.3.refs_5_
  21.4 0.0 collective-permute-done.2.refs_3_
  21.4 0.0 copy-done.1
  21.4 0.0 copy-done.5
  21.4 0.0 copy-done.4
  21.4 0.0 copy-done.3
  21.4 0.0 copy-done.2
  21.5 8.8 %atoms.1 = (bf16[4096,128]{1,0:T(8,128)(2,1)}, bf16[128,512]{1,0:T(8,128)(2,1)S(1)}, bf16[128,512]{1,0:T(8,128)(2,1)S(1)}, f32[128,512]{1,0:T(8,128)S(1)}) custom-call(s32[40,128]{1,0:T(8,128)S(1)} %get-tuple-element.12.refs_0_.refs_1_, s32[40,128]{1,0:T(8,128)S(1)} %get-tuple-element.12.refs_0_.refs_1_, bf16[4096,128]{1,0:T(8,128)(2,1)S(1)} %copy-done.1, ...), custom_call_target="tpu_custom_call" | custom-call | tf_op jit(solution)/shard_map/atoms/pallas_call | solution.py:323
  30.3 0.7 %collective-permute-start.4 = (bf16[128,512]{1,0:T(8,128)(2,1)S(1)}, bf16[128,512]{1,0:T(8,128)(2,1)S(1)}, u32[]{:S(2)}, u32[]{:S(2)}) collective-permute-start(bf16[128,512]{1,0:T(8,128)(2,1)S(1)} %get-tuple-element.15), channel_id=1, source_target_pairs={{0,1},{1,0},{2,3},{3,2},{4,5},{5,4},{6,7},{7,6},{8,9},{9,8},{10,11... | collective-permute-start | bytes 393224 | tf_op jit(solution)/shard_map/ppermute | solution.py:351
  30.9 2.1 %collective-permute-start.5 = (bf16[128,512]{1,0:T(8,128)(2,1)S(1)}, bf16[128,512]{1,0:T(8,128)(2,1)S(1)}, u32[]{:S(2)}, u32[]{:S(2)}) collective-permute-start(bf16[128,512]{1,0:T(8,128)(2,1)S(1)} %get-tuple-element.16), channel_id=1, source_target_pairs={{0,16},{1,2},{2,1},{3,4},{4,3},{5,6},{6,5},{7,8},{8,7},{9,10},{10,... | collective-permute-start | bytes 393224 | tf_op jit(solution)/shard_map/ppermute | solution.py:352
  33.1 2.2 %collective-permute-done.4 = bf16[128,512]{1,0:T(8,128)(2,1)S(1)} collective-permute-done((bf16[128,512]{1,0:T(8,128)(2,1)S(1)}, bf16[128,512]{1,0:T(8,128)(2,1)S(1)}, u32[]{:S(2)}, u32[]{:S(2)}) %collective-permute-start.4) | collective-permute-done | bytes 131104 | tf_op jit(solution)/shard_map/ppermute | solution.py:351
  35.3 2.7 %collective-permute-done.5 = bf16[128,512]{1,0:T(8,128)(2,1)S(1)} collective-permute-done((bf16[128,512]{1,0:T(8,128)(2,1)S(1)}, bf16[128,512]{1,0:T(8,128)(2,1)S(1)}, u32[]{:S(2)}, u32[]{:S(2)}) %collective-permute-start.5) | collective-permute-done | bytes 131104 | tf_op jit(solution)/shard_map/ppermute | solution.py:352
  38.0 0.0 copy-done
  38.0 0.0 copy-done.6
  38.0 1.3 %add_convert_fusion = bf16[512,768]{1,0:T(8,128)(2,1)} fusion(bf16[512,768]{1,0:T(8,128)(2,1)S(1)} %copy-done.6, bf16[128,768]{1,0:T(8,128)(2,1)S(1)} %copy-done, bf16[128,512]{1,0:T(8,128)(2,1)S(1)} %collective-permute-done.5, f32[128,512]{1,0:T(8,128)S(1)} %get-tuple-element.14, bf16[128,512]{1,0:T(8,128)(2,1)S(1)} %collective-permute-done.4, ...), kind=kOutput, calls=%fused_computation.1 | convolution fusion | flops 102236160 | bytes 2295808 | tf_op jit(solution)/shard_map/dot_general | solution.py:356
  (4 shorter events, 0.0 us)
Async XLA Ops:
  0.6 37.4 %copy-start = (bf16[128,768]{1,0:T(8,128)(2,1)S(1)}, bf16[128,768]{1,0:T(8,128)(2,1)}, u32[]{:S(2)}) copy-start(bf16[128,768]{1,0:T(8,128)(2,1)} %param.19) | copy-start | bytes 589828
  0.6 20.8 %copy-start.1 = (bf16[4096,128]{1,0:T(8,128)(2,1)S(1)}, bf16[4096,128]{1,0:T(8,128)(2,1)}, u32[]{:S(2)}) copy-start(bf16[4096,128]{1,0:T(8,128)(2,1)} %refs_2_.1) | copy-start | bytes 3145732
  0.7 5.5 %copy-start.7 = (s32[512]{0:T(512)S(1)}, s32[512]{0:T(512)}, u32[]{:S(2)}) copy-start(s32[512]{0:T(512)} %param.13) | copy-start | bytes 6148
  0.7 20.8 %copy-start.5 = (bf16[128,128]{1,0:T(8,128)(2,1)S(1)}, bf16[128,128]{1,0:T(8,128)(2,1)}, u32[]{:S(2)}) copy-start(bf16[128,128]{1,0:T(8,128)(2,1)} %refs_10_.1) | copy-start | bytes 98308
  0.7 20.8 %copy-start.4 = (bf16[128,128]{1,0:T(8,128)(2,1)S(1)}, bf16[128,128]{1,0:T(8,128)(2,1)}, u32[]{:S(2)}) copy-start(bf16[128,128]{1,0:T(8,128)(2,1)} %refs_9_.1) | copy-start | bytes 98308
  0.7 20.8 %copy-start.3 = (bf16[128,128]{1,0:T(8,128)(2,1)S(1)}, bf16[128,128]{1,0:T(8,128)(2,1)}, u32[]{:S(2)}) copy-start(bf16[128,128]{1,0:T(8,128)(2,1)} %refs_8_.1) | copy-start | bytes 98308
  0.7 20.8 %copy-start.2 = (bf16[128,128]{1,0:T(8,128)(2,1)S(1)}, bf16[128,128]{1,0:T(8,128)(2,1)}, u32[]{:S(2)}) copy-start(bf16[128,128]{1,0:T(8,128)(2,1)} %refs_7_.1) | copy-start | bytes 98308
  3.1 34.9 %copy-start.6 = (bf16[512,768]{1,0:T(8,128)(2,1)S(1)}, bf16[512,768]{1,0:T(8,128)(2,1)}, u32[]{:S(2)}) copy-start(bf16[512,768]{1,0:T(8,128)(2,1)} %param.11) | copy-start | bytes 2359300
  3.1 18.3 %collective-permute-start.3 = (bf16[640,128]{1,0:T(8,128)(2,1)S(1)}, bf16[640,128]{1,0:T(8,128)(2,1)S(1)}, u32[]{:S(2)}, u32[]{:S(2)}) collective-permute-start(bf16[640,128]{1,0:T(8,128)(2,1)S(1)} %pad_maximum_fusion.1), channel_id=1, source_target_pairs={{0,16},{1,2},{2,1},{3,4},{4,3},{5,6},{6,5},{7,8},{8,7},{9,10},{10,... | collective-permute-start | bytes 491528 | tf_op jit(solution)/shard_map/ppermute | solution.py:297
  5.8 15.6 %collective-permute-start.2 = (bf16[640,128]{1,0:T(8,128)(2,1)S(1)}, bf16[640,128]{1,0:T(8,128)(2,1)S(1)}, u32[]{:S(2)}, u32[]{:S(2)}) collective-permute-start(bf16[640,128]{1,0:T(8,128)(2,1)S(1)} %pad_maximum_fusion.1), channel_id=1, source_target_pairs={{0,1},{1,0},{2,3},{3,2},{4,5},{5,4},{6,7},{7,6},{8,9},{9,8},{10,11... | collective-permute-start | bytes 491528 | tf_op jit(solution)/shard_map/ppermute | solution.py:296
  6.8 13.0 %all-to-all-start = ((s32[16,4,128]{2,1,0:T(4,128)}), s32[16,4,128]{2,1,0:T(4,128)S(1)}, u32[]{:S(2)}, u32[]{:S(2)}) async-start(s32[16,4,128]{2,1,0:T(4,128)} %broadcast_in_dim.4), calls=%async_computation | async-start | bytes 65536 | tf_op jit(solution)/shard_map/all_to_all | solution.py:282
  30.3 5.1 %collective-permute-start.4 = (bf16[128,512]{1,0:T(8,128)(2,1)S(1)}, bf16[128,512]{1,0:T(8,128)(2,1)S(1)}, u32[]{:S(2)}, u32[]{:S(2)}) collective-permute-start(bf16[128,512]{1,0:T(8,128)(2,1)S(1)} %get-tuple-element.15), channel_id=1, source_target_pairs={{0,1},{1,0},{2,3},{3,2},{4,5},{5,4},{6,7},{7,6},{8,9},{9,8},{10,11... | collective-permute-start | bytes 393224 | tf_op jit(solution)/shard_map/ppermute | solution.py:351
  30.9 7.1 %collective-permute-start.5 = (bf16[128,512]{1,0:T(8,128)(2,1)S(1)}, bf16[128,512]{1,0:T(8,128)(2,1)S(1)}, u32[]{:S(2)}, u32[]{:S(2)}) collective-permute-start(bf16[128,512]{1,0:T(8,128)(2,1)S(1)} %get-tuple-element.16), channel_id=1, source_target_pairs={{0,16},{1,2},{2,1},{3,4},{4,3},{5,6},{6,5},{7,8},{8,7},{9,10},{10,... | collective-permute-start | bytes 393224 | tf_op jit(solution)/shard_map/ppermute | solution.py:352
